TPU v7x, 512 devices: a whole 4x8x8 slice. The times are simulated.
512 devices in a mesh: ctx: 64 (over x, y, core), heads: 8 (over z).
Axes of the slice: x: 4, y: 8, z: 8, core: 2. Of those that a mesh axis runs over, the one named last changes fastest.
Arguments:
- ssm_input: bfloat16 [12288, 8192], P('ctx', 'heads'), may hold values from -36 to 36
- gate_input: bfloat16 [12288, 8192], P('ctx', 'heads'), may hold values from -6 to 6
- write_proj: bfloat16 [12288, 128], P('ctx'), may hold values from -0.5 to 0.5
- read_proj: bfloat16 [12288, 128], P('ctx'), may hold values from -0.5 to 0.5
- log_decay: float32 [12288, 128], P('ctx', 'heads'), may hold values from -0.75 to 0, as said below
- skip_gain: float32 [128], P('heads'), may hold values from 0.5 to 2
- norm_gain: float32 [8192], P('heads'), may hold values from 0.1 to 1.9
- query_rows: bfloat16 [12288, 4096], P('ctx', 'heads'), may hold values from -6 to 6
- key_rows: bfloat16 [12288, 1024], P('ctx', 'heads'), may hold values from -6 to 6
- value_rows: bfloat16 [12288, 1024], P('ctx', 'heads'), may hold values from -6 to 6
Outputs:
- ssm_out: bfloat16 [12288, 8192], P('ctx', 'heads')
- attn_out: bfloat16 [12288, 4096], P('ctx', 'heads')
Inputs may be any that keep to these rules, and one draw needn't show every extreme that they name: `log_decay`: negative everywhere.
All inputs are finite; a program needn't handle non-finite values.
Results may differ from a plain program's by a relative error of at most 0.0075.
Values may be sent and summed in bfloat16 or wider, within the bound.
No kernel may reach another device: no remote copies, remote signals or barrier semaphores. Data moves between devices by JAX's collectives and lax.ppermute only.
A program may use at most 128 MiB of HBM per device.

v0:
```python
import jax
import jax.numpy as jnp
from jax import lax
from jax.sharding import PartitionSpec as P

SSM_HEADS = 128
HEAD_P = 64
STATE = 128
QUERY_HEADS = 32
KV_HEADS = 8
HEAD_DIM = 128
SPAN = 64


def carried_in(part, axis, combine, identity):
    place = lax.axis_index(axis)
    gathered = jax.tree.map(lambda a: lax.all_gather(a, axis), part)
    state = jax.tree.map(lambda a, e: jnp.zeros_like(a) + jnp.asarray(e, a.dtype), part, identity)

    def one(step, state):
        return combine(
            state, jax.tree.map(lambda a: lax.dynamic_index_in_dim(a, step, 0, False), gathered)
        )

    return lax.fori_loop(0, place, one, state)


def chain_combine(earlier, later):
    return (earlier[0] * later[0], later[0][:, None, None] * earlier[1] + later[1])


def local_mixer(ssm_input, gate_input, write_proj, read_proj, log_decay, skip_gain, norm_gain):
    row_count, width_local = ssm_input.shape
    head_local = log_decay.shape[1]
    block_count = row_count // SPAN
    inputs_blk = ssm_input.reshape(block_count, SPAN, head_local, HEAD_P)
    inputs_float = inputs_blk.astype(jnp.float32)
    write_blk = write_proj.reshape(block_count, SPAN, STATE)
    read_blk = read_proj.reshape(block_count, SPAN, STATE)
    cum_decay = jnp.cumsum(log_decay.reshape(block_count, SPAN, head_local), axis=1)
    cum_heads = jnp.transpose(cum_decay, (0, 2, 1))
    causal = jnp.arange(SPAN)[:, None] >= jnp.arange(SPAN)[None, :]
    decay_gap = cum_heads[:, :, :, None] - cum_heads[:, :, None, :]
    decay_mask = jnp.where(causal, jnp.exp(jnp.where(causal, decay_gap, 0.0)), 0.0)
    intersection = jnp.einsum(
        "ctn,csn->cts", read_blk, write_blk, preferred_element_type=jnp.float32
    )
    mix_weights = intersection[:, None] * decay_mask
    y_local = jnp.einsum(
        "chts,cshp->cthp", mix_weights, inputs_float, precision=lax.Precision.HIGHEST
    )
    tail_decay = jnp.exp(cum_heads[:, :, -1:] - cum_heads)
    weighted_write = tail_decay[:, :, :, None] * write_blk[:, None].astype(jnp.float32)
    block_state = jnp.einsum(
        "cshp,chsn->chpn", inputs_float, weighted_write, precision=lax.Precision.HIGHEST
    )
    block_decay = jnp.exp(cum_heads[:, :, -1])

    def prefix_step(carry_in, block_item):
        return (chain_combine(carry_in, block_item), carry_in)

    start_pair = (
        jnp.ones((head_local,), jnp.float32),
        jnp.zeros((head_local, HEAD_P, STATE), jnp.float32),
    )
    device_pair, prefix_pair = lax.scan(prefix_step, start_pair, (block_decay, block_state))
    incoming = carried_in(device_pair, "ctx", chain_combine, start_pair)
    start_state = prefix_pair[0][:, :, None, None] * incoming[1][None] + prefix_pair[1]
    y_carry = (
        jnp.einsum(
            "ctn,chpn->cthp",
            read_blk.astype(jnp.float32),
            start_state,
            precision=lax.Precision.HIGHEST,
        )
        * jnp.exp(cum_decay)[:, :, :, None]
    )
    mixed_out = y_local + y_carry + skip_gain[None, None, :, None] * inputs_float
    gated = mixed_out.reshape(row_count, width_local) * jax.nn.silu(gate_input.astype(jnp.float32))
    square_total = lax.psum(jnp.sum(gated * gated, axis=1), "heads")
    row_scale = lax.rsqrt(square_total / (SSM_HEADS * HEAD_P) + 1e-05)
    return (gated * row_scale[:, None] * norm_gain[None, :]).astype(jnp.bfloat16)


def attend_block(
    state, query_block, query_positions, top_position, key_block, value_block, first_key
):
    scale_factor = 1.0 / HEAD_DIM**0.5
    key_count = key_block.shape[0]

    def compute(state_in):
        running_max, running_sum, running_acc = state_in
        scores = (
            jnp.einsum("gqd,ngd->gqn", query_block, key_block, preferred_element_type=jnp.float32)
            * scale_factor
        )
        key_positions = first_key + jnp.arange(key_count, dtype=jnp.int32)
        visible = key_positions[None, None, :] <= query_positions[None, :, None]
        block_max = jnp.max(jnp.where(visible, scores, -1e30), axis=2)
        new_max = jnp.maximum(running_max, block_max)
        weights = jnp.where(
            visible, jnp.exp(jnp.where(visible, scores - new_max[:, :, None], 0.0)), 0.0
        )
        rescale = jnp.exp(running_max - new_max)
        new_sum = rescale * running_sum + jnp.sum(weights, axis=2)
        new_acc = rescale[:, :, None] * running_acc + jnp.einsum(
            "gqn,ngd->gqd",
            weights.astype(jnp.bfloat16),
            value_block,
            preferred_element_type=jnp.float32,
        )
        return (new_max, new_sum, new_acc)

    return lax.cond(first_key > top_position, lambda state_in: state_in, compute, state)


def attention_local(query_rows, key_rows, value_rows):
    row_count = query_rows.shape[0]
    head_sets = key_rows.shape[1] // HEAD_DIM
    group_size = QUERY_HEADS // KV_HEADS
    own_index = lax.axis_index("ctx")
    query_stack = query_rows.reshape(row_count, head_sets, group_size, HEAD_DIM)
    query_stack = jnp.transpose(query_stack, (1, 0, 2, 3)).reshape(
        head_sets, row_count * group_size, HEAD_DIM
    )
    stacked_rows = jnp.arange(row_count * group_size, dtype=jnp.int32) // group_size
    own_positions = own_index * row_count + stacked_rows
    query_sets = [(query_stack, own_positions)]
    tops = [jnp.max(positions) for _, positions in query_sets]
    carries = tuple(
        (
            (
                jnp.full((head_sets, block.shape[1]), -1e30, jnp.float32),
                jnp.zeros((head_sets, block.shape[1]), jnp.float32),
                jnp.zeros((head_sets, block.shape[1], HEAD_DIM), jnp.float32),
            )
            for block, _ in query_sets
        )
    )
    key_piece = lax.all_gather(key_rows, "ctx", axis=0, tiled=True)
    value_piece = lax.all_gather(value_rows, "ctx", axis=0, tiled=True)
    piece_rows = key_piece.shape[0]
    key_blocks = key_piece.reshape(piece_rows // row_count, row_count, head_sets, HEAD_DIM)
    value_blocks = value_piece.reshape(piece_rows // row_count, row_count, head_sets, HEAD_DIM)
    offsets = row_count * jnp.arange(piece_rows // row_count, dtype=jnp.int32)

    def inner_step(states, block_item):
        key_block, value_block, first_key = block_item
        updated = tuple(
            (
                attend_block(
                    states[number],
                    query_sets[number][0],
                    query_sets[number][1],
                    tops[number],
                    key_block,
                    value_block,
                    first_key,
                )
                for number in range(len(query_sets))
            )
        )
        return (updated, None)

    result, _ = lax.scan(inner_step, carries, (key_blocks, value_blocks, offsets))
    finished = [(state[2] / state[1][:, :, None]).astype(jnp.bfloat16) for state in result]
    combined = finished[0]
    combined = combined.reshape(head_sets, row_count, group_size, HEAD_DIM)
    return jnp.transpose(combined, (1, 0, 2, 3)).reshape(
        row_count, head_sets * group_size * HEAD_DIM
    )


def body(
    ssm_input,
    gate_input,
    write_proj,
    read_proj,
    log_decay,
    skip_gain,
    norm_gain,
    query_rows,
    key_rows,
    value_rows,
):
    ssm_out = local_mixer(
        ssm_input, gate_input, write_proj, read_proj, log_decay, skip_gain, norm_gain
    )
    attn_out = attention_local(query_rows, key_rows, value_rows)
    return (ssm_out, attn_out)


def solution(mesh):
    in_specs = (
        P("ctx", "heads"),
        P("ctx", "heads"),
        P("ctx", None),
        P("ctx", None),
        P("ctx", "heads"),
        P("heads"),
        P("heads"),
        P("ctx", "heads"),
        P("ctx", "heads"),
        P("ctx", "heads"),
    )
    out_specs = (P("ctx", "heads"), P("ctx", "heads"))
    return jax.shard_map(body, mesh=mesh, in_specs=in_specs, out_specs=out_specs, check_vma=False)
```

profile of v0, /device:TPU:63, one launch (start us, length us, event | category | flops | bytes accessed | tf_op | source)
XLA Modules:
  0.0 625.4 jit_solution(15439639091845416310)
XLA Ops:
  13.1 6.8 %while.46 = (s32[]{:T(128)}, f32[16]{0:T(128)S(1)}, f32[16,64,128]{2,1,0:T(8,128)S(1)}, f32[3,16]{1,0:T(4,128)}, f32[3,16,64,128]{3,2,1,0:T(8,128)}, /*index=5*/...) while((s32[]{:T(128)}, f32[16]{0:T(128)S(1)}, ...), condition=%wide.region_2.3_spmd.clone, body=%wide.region_1.2_spmd.clone.sunk | while | flops 524323 | bytes 2622581 | solution.py:66
  23.0 124.2 %all-reduce = f32[1024]{0:T(1024)S(1)} all-reduce(f32[1024]{0:T(1024)S(1)} %dynamic-update-slice), channel_id=2, replica_groups=mesh['ctx'=64,'heads'=8] {'ctx'}, use_global_device_ids=true, to_apply=%add | all-reduce | flops 1024 | bytes 8192
  148.4 33.0 %all-gather.8.cloned.1.call-done = bf16[12288,128]{1,0:T(8,128)(2,1)} async-done(((bf16[192,128]{1,0:T(8,128)(2,1)}), bf16[12288,128]{1,0:T(8,128)(2,1)}) %all-gather.8.cloned.1.call-update) | async-done | bytes 3145744 | tf_op jit(solution)/shard_map/all_gather | solution.py:141
  181.4 336.1 %while.45 = (s32[]{:T(128)}, f32[1,768]{1,0:T(1,128)S(1)}, f32[1,768]{1,0:T(1,128)S(1)}, f32[1,768,128]{2,1,0:T(8,128)S(1)}, s32[64]{0:T(128)S(1)}, /*index=5*/s...) while((s32[]{:T(128)}, f32[1,768]{1,0:T(1,128)S(1)}, ...), condition=%wide.region_13.14_spmd.clone, body=%wide.region_8.13_spmd.clone.sunk | while | flops 77767872 | bytes 2938171 | solution.py:165
  183.4 3.3 conditional.3
  188.6 3.3 conditional.3
  199.1 3.3 conditional.3
  204.4 3.3 conditional.3
  209.6 3.3 conditional.3
  220.1 3.3 conditional.3
  251.6 3.3 conditional.3
  256.9 3.3 conditional.3
  262.1 3.3 conditional.3
  267.4 3.3 conditional.3
  272.7 3.3 conditional.3
  277.9 3.3 conditional.3
  283.2 3.3 conditional.3
  288.5 3.3 conditional.3
  293.7 3.3 conditional.3
  299.0 3.3 conditional.3
  309.5 3.3 conditional.3
  314.7 3.3 conditional.3
  518.6 78.0 %while.44 = (s32[]{:T(128)}, f32[16,64,128]{2,1,0:T(8,128)S(1)}, s32[]{:T(128)}, f32[64,16]{1,0:T(8,128)S(1)}, f32[64,16,64,128]{3,2,1,0:T(8,128)}, /*index=5*/s32[]{:T(128)}, s32[]{:T(128)}, s32[]{:T(128)}) while((s32[]{:T(128)}, f32[16,64,128]{2,1,0:T(8,128)S(1)}, s32[]{:T(128)}, f32[64,16]{1,0:T(8,128)S(1)}, f32[64,16,64,128]{3,2,1,0:T(8,128)}, ...), condition=%wide.region_4.5_spmd, body=%wide.region_3.4_spmd.sunk | while | flops 262149 | bytes 1573183 | solution.py:25
  603.3 14.5 %psum.7 = f32[192]{0:T(256)S(1)} all-reduce(f32[192]{0:T(256)S(1)} %multiply_reduce_fusion), channel_id=1, replica_groups=mesh['ctx'=64,'heads'=8] {'heads'}, use_global_device_ids=true, to_apply=%region_6.7 | all-reduce | flops 192 | bytes 1536 | tf_op jit(solution)/shard_map/psum | solution.py:80
  (952 shorter events, 503.4 us)
Async XLA Ops:
  7.2 141.0 %copy-start = (bf16[192,128]{1,0:T(8,128)(2,1)S(1)}, bf16[192,128]{1,0:T(8,128)(2,1)}, u32[]{:S(2)}) copy-start(bf16[192,128]{1,0:T(8,128)(2,1)} %param.21) | copy-start | bytes 147460
  7.2 4.2 copy-start.5
  7.2 141.2 %all-gather.6.cloned.1.call-start = ((), (), s32[]{:S(2)}) async-start(), calls=%async_computation | async-start | bytes 3194880 | tf_op jit(solution)/shard_map/all_gather | solution.py:140
  7.9 173.5 %all-gather.8.cloned.1.call-start = ((), (), s32[]{:S(2)}) async-start(), calls=%async_computation.1 | async-start | bytes 3194880 | tf_op jit(solution)/shard_map/all_gather | solution.py:141
  8.7 509.9 %all-gather.10.cloned.1.call-start = ((), (), s32[]{:S(2)}) async-start(), calls=%async_computation.2 | async-start | bytes 34078720 | tf_op jit(solution)/shard_map/all_gather | solution.py:17
  13.1 134.2 %copy-start.4 = (bf16[192,512]{1,0:T(8,128)(2,1)S(1)}, bf16[192,512]{1,0:T(8,128)(2,1)}, u32[]{:S(2)}) copy-start(bf16[192,512]{1,0:T(8,128)(2,1)} %param.25) | copy-start | bytes 589828
  20.0 0.8 copy-start.1
  518.6 78.1 %copy-start.2 = (f32[3,16,64,128]{3,2,1,0:T(8,128)S(1)}, f32[3,16,64,128]{3,2,1,0:T(8,128)}, u32[]{:S(2)}) copy-start(f32[3,16,64,128]{3,2,1,0:T(8,128)} %get-tuple-element.226) | copy-start | bytes 4718596
  518.6 78.1 %copy-start.7 = (f32[3,16]{1,0:T(4,128)S(1)}, f32[3,16]{1,0:T(4,128)}, u32[]{:S(2)}) copy-start(f32[3,16]{1,0:T(4,128)} %get-tuple-element.222) | copy-start | bytes 580
  596.7 2.5 copy-start.8
  602.0 1.0 copy-start.3
  602.0 15.8 %copy-start.6 = (f32[1024]{0:T(1024)S(1)}, f32[1024]{0:T(1024)}, u32[]{:S(2)}) copy-start(f32[1024]{0:T(1024)} %param.24) | copy-start | bytes 12292
Sparse Core Ops, SparseCore 0:
  11.4 85.3 all-gather.5
  100.1 81.2 all-gather.7
  184.8 144.7 all-gather.9
where the time goes:
time: 637 us; the launch traced here: 625 us
  matrix products  157 us (25%)
  blocking collectives  139 us (22%)
  other arithmetic  138 us (22%)
  loops' own time  88.4 us (14%)
  local copies, waits for them, and re-layouts  54.1 us (8%)
  waiting for transfers between devices  34.4 us (5%)
  between operations  14.7 us (2%)
    unnamed x1, blocking collectives  124 us
    dot_general x64, matrix products, compute(): jnp.einsum('gqn,ngd->gqd', weights.astype(jnp.bfloat16), value_block, pre...  83.3 us
    another operation x1, loops' own time, attention_local(): lax.scan(inner_step, carries, (key_blocks, value_blocks, offsets))  81.8 us
    add x66, other arithmetic, chain_combine(): later[0][:, None, None] * earlier[1] + later[1]  75.3 us
    dot_general x64, matrix products, compute(): jnp.einsum('gqd,ngd->gqn', query_block, key_block, preferred_element_type...  68.2 us
    dynamic_slice x64, local copies, waits for them, and re-layouts, attention_local(): lax.scan(inner_step, carries, (key_blocks, value_blocks, offsets))  41.2 us
    add x64, other arithmetic, compute(): key_positions = first_key + jnp.arange(key_count, dtype=jnp.int32)  39.9 us
    all_gather x1, waiting for transfers between devices, attention_local(): value_piece = lax.all_gather(value_rows, 'ctx', axis=0, tiled=True)  33 us
  transfers between devices with their start and end apart: 3, of which 1 were waited for; matrix products, arithmetic and copies ran while one was open for 42% of the time, Pallas kernels for 0%

commit v1 on v0

v1 whole, which is shorter than its diff:
```python
import functools

import jax
import jax.numpy as jnp
from jax import lax
from jax.experimental import pallas as pl
from jax.experimental.pallas import tpu as pltpu
from jax.sharding import PartitionSpec as P

SSM_HEADS = 128
HEAD_P = 64
STATE = 128
HEAD_DIM = 128
PLACES = 64
LANES = 128
KEYS = 768
HIGH = lax.Precision.HIGHEST
F32 = jnp.float32
BF16 = jnp.bfloat16
VMEM_LIMIT = 48 * 1024 * 1024


def dot(a, b, ca, cb, precision=None):
    return lax.dot_general(
        a, b, (((ca,), (cb,)), ((), ())), precision=precision, preferred_element_type=F32
    )


def head_expansion(heads, width):
    row = lax.broadcasted_iota(jnp.int32, (heads, width), 0)
    col = lax.broadcasted_iota(jnp.int32, (heads, width), 1)
    return (col // HEAD_P == row).astype(F32)


def lower_mask(rows):
    t = lax.broadcasted_iota(jnp.int32, (rows, rows), 0)
    s = lax.broadcasted_iota(jnp.int32, (rows, rows), 1)
    return t >= s


def state_kernel(x_ref, write_ref, decay_ref, out_ref):
    rows, width = x_ref.shape
    heads = decay_ref.shape[1]
    share = width // PLACES
    decay = decay_ref[...]
    later = (~lower_mask(rows)).astype(F32)
    tail = jnp.exp(dot(later, decay, 1, 0, HIGH))
    tail = dot(tail, head_expansion(heads, width), 1, 0, HIGH)
    scaled = (x_ref[...].astype(F32) * tail).astype(BF16)
    state = dot(scaled, write_ref[...], 0, 0)
    out_ref[:, 0:share, :] = state.reshape(PLACES, share, STATE).astype(BF16)
    total = dot(decay, jnp.ones((rows, LANES), F32), 0, 0, HIGH)
    high = total.astype(BF16).astype(F32)
    middle = (total - high).astype(BF16).astype(F32)
    low = (total - high - middle).astype(BF16).astype(F32)
    row = lax.broadcasted_iota(jnp.int32, (heads, 8, LANES), 1)
    pieces = jnp.where(
        row == 0,
        high[:, None, :],
        jnp.where(row == 1, middle[:, None, :], jnp.where(row == 2, low[:, None, :], 0.0)),
    )
    pieces = jnp.broadcast_to(pieces[:, None], (heads, PLACES // heads, 8, LANES))
    out_ref[:, share : share + 8, :] = pieces.reshape(PLACES, 8, LANES).astype(BF16)


def fold_kernel(parts_ref, out_ref):
    places, deep, lanes = parts_ref.shape
    share = deep - 8
    state = jnp.zeros((share, lanes), F32)
    for i in range(places):
        out_ref[i] = state.astype(BF16)
        if i + 1 < places:
            part = parts_ref[i].astype(F32)
            total = part[share : share + 1] + part[share + 1 : share + 2]
            total = total + part[share + 2 : share + 3]
            state = state * jnp.exp(total) + part[0:share]


def mixer_kernel(
    x_ref, gate_ref, write_ref, read_ref, decay_ref, skip_ref, start_ref, gated_ref, square_ref
):
    rows, width = x_ref.shape
    heads = decay_ref.shape[1]
    mask = lower_mask(rows)
    lower = mask.astype(F32)
    decay = decay_ref[...]
    cum = dot(lower, decay, 1, 0, HIGH)
    cum_heads = dot(decay, lower, 0, 1, HIGH)
    expansion = head_expansion(heads, width)
    grown = dot(jnp.exp(cum), expansion, 1, 0, HIGH)
    skip = dot(skip_ref[...], expansion, 1, 0, HIGH)[0:1]
    gain = dot(read_ref[...], write_ref[...], 1, 1)
    carry = dot(read_ref[...], start_ref[...], 1, 1)
    lane = lax.broadcasted_iota(jnp.int32, (rows, LANES), 1)
    total = jnp.zeros((8, rows), F32)
    for pair in range(width // LANES):
        cols = slice(pair * LANES, (pair + 1) * LANES)
        x = x_ref[:, cols]
        found = []
        for h in (2 * pair, 2 * pair + 1):
            gap = cum[:, h : h + 1] - cum_heads[h : h + 1, :]
            mix = gain * jnp.exp(jnp.where(mask, gap, -1e30))
            found.append(dot(mix.astype(BF16), x, 1, 0))
        mixed = jnp.where(lane < HEAD_P, found[0], found[1])
        mixed = mixed + carry[:, cols] * grown[:, cols] + skip[:, cols] * x.astype(F32)
        gate = gate_ref[:, cols].astype(F32)
        gated = mixed * (gate / (1.0 + jnp.exp(-gate)))
        gated_ref[:, cols] = gated
        total = total + dot(jnp.ones((8, LANES), F32), gated * gated, 1, 1, HIGH)
    square_ref[...] = total


def norm_kernel(gated_ref, square_ref, gain_ref, out_ref):
    total = dot(square_ref[...], jnp.ones((square_ref.shape[0], LANES), F32), 0, 0, HIGH)
    scale = lax.rsqrt(total / (SSM_HEADS * HEAD_P) + 1e-05)
    for c in range(0, out_ref.shape[1], LANES):
        cols = slice(c, c + LANES)
        out_ref[:, cols] = (gated_ref[:, cols] * scale * gain_ref[:, cols]).astype(BF16)


def attention_kernel(place_ref, query_ref, kv_ref, out_ref, kv, top, acc, sems):
    rows, width = query_ref.shape
    sets = width // HEAD_DIM
    factor = 1.4426950408889634 / HEAD_DIM**0.5
    place = place_ref[0]
    last = (place * rows) // KEYS

    def fetch(c):
        span = pl.ds(pl.multiple_of(c * KEYS, KEYS), KEYS)
        return pltpu.make_async_copy(kv_ref.at[span], kv.at[span], sems.at[c])

    @pl.loop(0, last + 1)
    def _(c):
        fetch(c).start()

    top[...] = jnp.full(top.shape, -1e30, F32)
    acc[...] = jnp.zeros(acc.shape, F32)

    def step(c, diagonal):
        fetch(c).wait()
        span = pl.ds(pl.multiple_of(c * KEYS, KEYS), KEYS)
        keys = kv[span, 0:HEAD_DIM]
        values = jnp.concatenate(
            [kv[span, HEAD_DIM : 2 * HEAD_DIM], jnp.ones((KEYS, LANES), BF16)], axis=1
        )
        if diagonal:
            t = lax.broadcasted_iota(jnp.int32, (rows, KEYS), 0) + place * rows
            s = lax.broadcasted_iota(jnp.int32, (rows, KEYS), 1) + c * KEYS
            visible = s <= t
        for j in range(sets):
            here = slice(j * rows, (j + 1) * rows)
            scores = dot(query_ref[:, j * HEAD_DIM : (j + 1) * HEAD_DIM], keys, 1, 1)
            if diagonal:
                scores = jnp.where(visible, scores, -1e30)
            old = top[here, 0:1]
            new = jnp.maximum(old, jnp.max(scores, axis=1, keepdims=True))
            weights = jnp.exp2((scores - new) * factor).astype(BF16)
            acc[here] = acc[here] * jnp.exp2((old - new) * factor) + dot(weights, values, 1, 0)
            top[here] = jnp.broadcast_to(new, (rows, LANES))

    @pl.loop(0, last)
    def _(c):
        step(c, False)

    step(last, True)
    for j in range(sets):
        here = slice(j * rows, (j + 1) * rows)
        out_ref[:, j * HEAD_DIM : (j + 1) * HEAD_DIM] = (
            acc[here, 0:HEAD_DIM] / acc[here, HEAD_DIM : 2 * HEAD_DIM]
        ).astype(BF16)


def vmem_call(kernel, outs, name, flops, moved, **more):
    return pl.pallas_call(
        kernel,
        out_shape=outs,
        name=name,
        compiler_params=pltpu.CompilerParams(vmem_limit_bytes=VMEM_LIMIT),
        cost_estimate=pl.CostEstimate(flops=flops, bytes_accessed=moved, transcendentals=0),
        **more,
    )


def body(
    ssm_input,
    gate_input,
    write_proj,
    read_proj,
    log_decay,
    skip_gain,
    norm_gain,
    query_rows,
    key_rows,
    value_rows,
):
    rows, width = ssm_input.shape
    heads = log_decay.shape[1]
    share = width // PLACES
    place = lax.axis_index("ctx").astype(jnp.int32).reshape(1)

    kv = lax.all_gather(
        jnp.concatenate([key_rows, value_rows], axis=1), "ctx", axis=0, tiled=True
    )

    parts = vmem_call(
        state_kernel,
        jax.ShapeDtypeStruct((PLACES, share + 8, STATE), BF16),
        "device_state",
        2 * rows * width * STATE,
        2 * rows * width,
    )(ssm_input, write_proj, log_decay)
    parts = lax.all_to_all(parts, "ctx", 0, 0, tiled=True)
    starts = vmem_call(
        fold_kernel,
        jax.ShapeDtypeStruct((PLACES, share, STATE), BF16),
        "state_fold",
        2 * width * STATE,
        4 * width * STATE,
    )(parts)
    starts = lax.all_to_all(starts, "ctx", 0, 0, tiled=True)
    gated, square = vmem_call(
        mixer_kernel,
        (
            jax.ShapeDtypeStruct((rows, width), F32),
            jax.ShapeDtypeStruct((8, rows), F32),
        ),
        "mixer",
        4 * rows * rows * width,
        12 * rows * width,
    )(
        ssm_input,
        gate_input,
        write_proj,
        read_proj,
        log_decay,
        jnp.broadcast_to(skip_gain[None], (8, heads)),
        starts.reshape(width, STATE),
    )
    square = lax.all_to_all(square, "heads", 0, 0, tiled=True)
    ssm_out = vmem_call(
        norm_kernel,
        jax.ShapeDtypeStruct((rows, width), BF16),
        "norm",
        4 * rows * width,
        6 * rows * width,
    )(gated, square, norm_gain[None])

    length = kv.shape[0]
    attn_out = vmem_call(
        attention_kernel,
        jax.ShapeDtypeStruct(query_rows.shape, BF16),
        "attention",
        2 * rows * 4 * length * 2 * HEAD_DIM,
        2 * length * 2 * HEAD_DIM,
        in_specs=[
            pl.BlockSpec(memory_space=pltpu.SMEM),
            pl.BlockSpec(memory_space=pltpu.VMEM),
            pl.BlockSpec(memory_space=pl.ANY),
        ],
        out_specs=pl.BlockSpec(memory_space=pltpu.VMEM),
        scratch_shapes=[
            pltpu.VMEM((length, 2 * HEAD_DIM), BF16),
            pltpu.VMEM((4 * rows, LANES), F32),
            pltpu.VMEM((4 * rows, 2 * HEAD_DIM), F32),
            pltpu.SemaphoreType.DMA((length // KEYS,)),
        ],
    )(place, query_rows, kv)
    return (ssm_out, attn_out)


def solution(mesh):
    split = P("ctx", "heads")
    in_specs = (
        split,
        split,
        P("ctx", None),
        P("ctx", None),
        split,
        P("heads"),
        P("heads"),
        split,
        split,
        split,
    )
    return jax.shard_map(
        body, mesh=mesh, in_specs=in_specs, out_specs=(split, split), check_vma=False
    )
```

time: 637 us -> 133 us (0.21); the launches traced: 625 us -> 132 us
  matrix products: 157 us -> 0 us
  other arithmetic: 138 us -> 1.48 us
  blocking collectives: 139 us -> 39.9 us
  loops' own time: 88.4 us -> 0 us
  local copies, waits for them, and re-layouts: 54.1 us -> 9.11 us
  Pallas kernels: 0 us -> 31.6 us
  starting transfers between devices: 0.11 us -> 11.2 us
  waiting for transfers between devices: 34.4 us -> 24.8 us
    dot_general x132 -> x0, matrix products: 157 us -> none  [the longest x64 83.3 us: compute(): jnp.einsum('gqn,ngd->gqd', weights.astype(jnp.bfloat16), value_block, pre...]
    unnamed x1 -> x0, blocking collectives: 124 us -> none
    add x258 -> x0, other arithmetic: 117 us -> none  [the longest x66 75.3 us: chain_combine(): later[0][:, None, None] * earlier[1] + later[1]]
    another operation x67 -> x0, loops' own time: 88.4 us -> none  [the longest x1 81.8 us: attention_local(): lax.scan(inner_step, carries, (key_blocks, value_blocks, offsets))]
    dynamic_slice x64 -> x0, local copies, waits for them, and re-layouts: 41.2 us -> none  [attention_local(): lax.scan(inner_step, carries, (key_blocks, value_blocks, offsets))]
    all_to_all x0 -> x2, blocking collectives: none -> 39.9 us  [the longest x1 21.4 us: body(): parts = lax.all_to_all(parts, 'ctx', 0, 0, tiled=True)]
    pallas_call x0 -> x5, Pallas kernels: none -> 31.6 us  [the longest x1 23.7 us: body(): vmem_call(attention_kernel, jax.ShapeDtypeStruct(query_rows.shape, BF16),...]
    all_gather x3 -> x1, waiting for transfers between devices: 33 us -> 18.2 us  [body(): lax.all_gather(jnp.concatenate([key_rows, value_rows], axis=1), 'ctx', ax...]
  transfers between devices with their start and end apart: 3 -> 2, of which waited for: 1 -> 2; matrix products, arithmetic and copies ran while one was open for 42% -> 2% of each run, Pallas kernels for 0% -> 6%
where the time goes in v1:
time: 133 us; the launch traced here: 132 us
  blocking collectives  39.9 us (30%)
  Pallas kernels  31.6 us (24%)
  waiting for transfers between devices  24.8 us (19%)
  between operations  14.1 us (11%)
  starting transfers between devices  11.2 us (8%)
  local copies, waits for them, and re-layouts  9.11 us (7%)
  other arithmetic  1.48 us (1%)
    pallas_call x1, Pallas kernels, body(): vmem_call(attention_kernel, jax.ShapeDtypeStruct(query_rows.shape, BF16),...  23.7 us
    all_to_all x1, blocking collectives, body(): parts = lax.all_to_all(parts, 'ctx', 0, 0, tiled=True)  21.4 us
    all_to_all x1, blocking collectives, body(): starts = lax.all_to_all(starts, 'ctx', 0, 0, tiled=True)  18.5 us
    all_gather x1, waiting for transfers between devices, body(): lax.all_gather(jnp.concatenate([key_rows, value_rows], axis=1), 'ctx', ax...  18.2 us
    all_to_all x1, starting transfers between devices, body(): square = lax.all_to_all(square, 'heads', 0, 0, tiled=True)  11.1 us
    unnamed x18, local copies, waits for them, and re-layouts  7.81 us
    all_to_all x1, waiting for transfers between devices, body(): square = lax.all_to_all(square, 'heads', 0, 0, tiled=True)  6.58 us
    pallas_call x1, Pallas kernels, body(): vmem_call(mixer_kernel, (jax.ShapeDtypeStruct((rows, width), F32), jax.Sh...  4.79 us
  transfers between devices with their start and end apart: 2, of which 2 were waited for; matrix products, arithmetic and copies ran while one was open for 2% of the time, Pallas kernels for 6%

profile of v1, /device:TPU:63, one launch (start us, length us, event | category | flops | bytes accessed | tf_op | source)
XLA Modules:
  0.0 132.2 jit_solution(8486970437305951259)
XLA Ops:
  7.2 0.0 all-gather.2.cloned.1.call-start
  7.2 1.5 %pad_maximum_fusion = bf16[192,256]{1,0:T(8,128)(2,1)} fusion(bf16[192,128]{1,0:T(8,128)(2,1)} %param.19, bf16[192,128]{1,0:T(8,128)(2,1)} %param.18), kind=kLoop, calls=%fused_computation | loop fusion | flops 196608 | bytes 196608 | tf_op jit(solution)/shard_map/concatenate | solution.py:202
  8.7 0.0 all-gather.2.cloned.1.call-update
  8.7 0.8 copy.15.decay_ref
  9.5 1.0 copy-done
  10.5 0.8 copy-done.3
  11.3 1.9 %device_state.1 = bf16[64,24,128]{2,1,0:T(8,128)(2,1)S(1)} custom-call(bf16[192,1024]{1,0:T(8,128)(2,1)S(1)} %copy-done, bf16[192,128]{1,0:T(8,128)(2,1)S(1)} %copy-done.3, f32[192,16]{1,0:T(8,128)S(1)} %copy.15.decay_ref), custom_call_target="tpu_custom_call" | custom-call | flops 50331648 | bytes 393216 | tf_op jit(solution)/shard_map/device_state/pallas_call | solution.py:205
  13.2 21.4 %all_to_all.21.parts_ref = bf16[64,24,128]{2,1,0:T(8,128)(2,1)S(1)} all-to-all(bf16[64,24,128]{2,1,0:T(8,128)(2,1)S(1)} %device_state.1), channel_id=1, replica_groups=mesh['ctx'=64,'heads'=8] {'ctx'}, dimensions={0} | all-to-all | bytes 786432 | tf_op jit(solution)/shard_map/all_to_all | solution.py:212
  34.6 0.1 state_fold.1
  34.7 18.5 %all_to_all.22 = bf16[64,16,128]{2,1,0:T(8,128)(2,1)S(1)} all-to-all(bf16[64,16,128]{2,1,0:T(8,128)(2,1)S(1)} %state_fold.1), channel_id=1, replica_groups=mesh['ctx'=64,'heads'=8] {'ctx'}, dimensions={0} | all-to-all | bytes 524288 | tf_op jit(solution)/shard_map/all_to_all | solution.py:220
  53.3 0.7 broadcast_in_dim.4.skip_ref
  53.9 1.0 copy-done.1
  54.9 1.0 copy-done.2
  55.9 0.8 copy-done.4
  56.7 0.8 copy-done.5
  57.5 4.8 %mixer.1 = (f32[192,1024]{1,0:T(8,128)S(1)}, f32[8,192]{1,0:T(8,128)S(1)}) custom-call(bf16[192,1024]{1,0:T(8,128)(2,1)S(1)} %copy-done.1, bf16[192,1024]{1,0:T(8,128)(2,1)S(1)} %copy-done.2, bf16[192,128]{1,0:T(8,128)(2,1)S(1)} %copy-done.4, bf16[192,128]{1,0:T(8,128)(2,1)S(1)} %copy-done.5, f32[192,16]{1,0:T(8,128)S(1)} %copy.15.decay_ref, ...), custom_call_target="tpu_custom_call" | custom-call | flops 150994944 | bytes 2359296 | tf_op jit(solution)/shard_map/mixer/pallas_call | solution.py:221
  62.3 0.6 copy.16
  63.0 11.1 %all-to-all-start.2 = ((f32[8,1,192]{2,1,0:T(1,128)}), f32[8,1,192]{2,1,0:T(1,128)S(1)}, u32[]{:S(2)}, u32[]{:S(2)}) async-start(f32[8,1,192]{2,1,0:T(1,128)} %copy.16), calls=%async_computation.2 | async-start | bytes 16384 | tf_op jit(solution)/shard_map/all_to_all | solution.py:239
  74.1 6.6 %all-to-all-done.2 = f32[8,1,192]{2,1,0:T(1,128)S(1)} async-done(((f32[8,1,192]{2,1,0:T(1,128)}), f32[8,1,192]{2,1,0:T(1,128)S(1)}, u32[]{:S(2)}, u32[]{:S(2)}) %all-to-all-start.2) | async-done | bytes 6176 | tf_op jit(solution)/shard_map/all_to_all | solution.py:239
  80.7 0.7 copy-done.6
  81.4 1.1 norm.1
  82.5 18.2 %all-gather.2.cloned.1.call-done.kv_ref = bf16[12288,256]{1,0:T(8,128)(2,1)} async-done(((bf16[192,256]{1,0:T(8,128)(2,1)}), bf16[12288,256]{1,0:T(8,128)(2,1)}) %all-gather.2.cloned.1.call-update) | async-done | bytes 6291472 | tf_op jit(solution)/shard_map/all_gather | solution.py:201
  100.7 0.9 copy-done.7
  101.6 23.7 %attention.1 = bf16[192,512]{1,0:T(8,128)(2,1)} custom-call(s32[1]{0:T(128)} %bitcast.3.place_ref, bf16[192,512]{1,0:T(8,128)(2,1)S(1)} %copy-done.7, bf16[12288,256]{1,0:T(8,128)(2,1)} %all-gather.2.cloned.1.call-done.kv_ref), custom_call_target="tpu_custom_call" | custom-call | flops 4831838208 | bytes 6291456 | tf_op jit(solution)/shard_map/attention/pallas_call | solution.py:249
  (9 shorter events, 0.0 us)
Async XLA Ops:
  7.2 93.6 %all-gather.2.cloned.1.call-start = ((), (), s32[]{:S(2)}) async-start(), calls=%async_computation.3 | async-start | bytes 6389760 | tf_op jit(solution)/shard_map/all_gather | solution.py:201
  9.5 1.0 copy-start
  10.5 0.8 copy-start.3
  53.9 1.0 copy-start.1
  54.9 1.0 copy-start.2
  55.9 0.8 copy-start.4
  56.7 0.8 copy-start.5
  63.0 17.7 %all-to-all-start.2 = ((f32[8,1,192]{2,1,0:T(1,128)}), f32[8,1,192]{2,1,0:T(1,128)S(1)}, u32[]{:S(2)}, u32[]{:S(2)}) async-start(f32[8,1,192]{2,1,0:T(1,128)} %copy.16), calls=%async_computation.2 | async-start | bytes 16384 | tf_op jit(solution)/shard_map/all_to_all | solution.py:239
  80.7 0.7 copy-start.6
  100.7 0.9 copy-start.7
Sparse Core Ops, SparseCore 0:
  11.9 88.7 all-gather.1

commit v2 on v1

v2 whole, which is shorter than its diff:
```python
import jax
import jax.numpy as jnp
from jax import lax
from jax.experimental import pallas as pl
from jax.experimental.pallas import tpu as pltpu
from jax.sharding import Mesh
from jax.sharding import PartitionSpec as P

SSM_HEADS = 128
HEAD_P = 64
STATE = 128
HEAD_DIM = 128
PLACES = 64
LANES = 128
GROUP = 16
CTX = ("x", "y", "core")
HIGH = lax.Precision.HIGHEST
F32 = jnp.float32
BF16 = jnp.bfloat16
VMEM_LIMIT = 48 * 1024 * 1024


def dot(a, b, ca, cb, precision=None):
    return lax.dot_general(
        a, b, (((ca,), (cb,)), ((), ())), precision=precision, preferred_element_type=F32
    )


def head_expansion(heads, width):
    row = lax.broadcasted_iota(jnp.int32, (heads, width), 0)
    col = lax.broadcasted_iota(jnp.int32, (heads, width), 1)
    return (col // HEAD_P == row).astype(F32)


def lower_mask(rows):
    t = lax.broadcasted_iota(jnp.int32, (rows, rows), 0)
    s = lax.broadcasted_iota(jnp.int32, (rows, rows), 1)
    return t >= s


def fetch_all(pairs, sems):
    copies = [pltpu.make_async_copy(a, b, sems.at[i]) for i, (a, b) in enumerate(pairs)]
    for copy in copies:
        copy.start()
    return copies


def state_kernel(decay_hbm, x_hbm, write_hbm, out_ref, decay_ref, x_ref, write_ref, sems):
    copies = fetch_all([(decay_hbm, decay_ref), (x_hbm, x_ref), (write_hbm, write_ref)], sems)
    copies[0].wait()
    rows, width = x_ref.shape
    heads = decay_ref.shape[0]
    share = width // PLACES
    decay = decay_ref[...]
    later = (~lower_mask(rows)).astype(F32)
    tail = jnp.exp(dot(later, decay, 1, 1, HIGH))
    tail = dot(tail, head_expansion(heads, width), 1, 0, HIGH)
    total = dot(decay, jnp.ones((rows, LANES), F32), 1, 0, HIGH)
    high = total.astype(BF16).astype(F32)
    middle = (total - high).astype(BF16).astype(F32)
    low = (total - high - middle).astype(BF16).astype(F32)
    row = lax.broadcasted_iota(jnp.int32, (heads, 8, LANES), 1)
    pieces = jnp.where(
        row == 0,
        high[:, None, :],
        jnp.where(row == 1, middle[:, None, :], jnp.where(row == 2, low[:, None, :], 0.0)),
    )
    pieces = jnp.broadcast_to(pieces[:, None], (heads, PLACES // heads, 8, LANES))
    out_ref[:, share : share + 8, :] = pieces.reshape(PLACES, 8, LANES).astype(BF16)
    copies[1].wait()
    copies[2].wait()
    scaled = (x_ref[...].astype(F32) * tail).astype(BF16)
    state = dot(scaled, write_ref[...], 0, 0)
    out_ref[:, 0:share, :] = state.reshape(PLACES, share, STATE).astype(BF16)


def fold_kernel(parts_ref, out_ref):
    places, deep, lanes = parts_ref.shape
    share = deep - 8
    state = jnp.zeros((share, lanes), F32)
    for i in range(places):
        out_ref[i] = state.astype(BF16)
        if i + 1 < places:
            part = parts_ref[i].astype(F32)
            total = part[share : share + 1] + part[share + 1 : share + 2]
            total = total + part[share + 2 : share + 3]
            state = state * jnp.exp(total) + part[0:share]


def mixer_kernel(
    x_hbm,
    gate_hbm,
    write_hbm,
    read_hbm,
    decay_hbm,
    skip_ref,
    start_ref,
    gated_ref,
    square_ref,
    decay_ref,
    x_ref,
    gate_ref,
    write_ref,
    read_ref,
    sems,
):
    copies = fetch_all(
        [
            (decay_hbm, decay_ref),
            (read_hbm, read_ref),
            (write_hbm, write_ref),
            (x_hbm, x_ref),
            (gate_hbm, gate_ref),
        ],
        sems,
    )
    copies[0].wait()
    rows, width = x_ref.shape
    heads = decay_ref.shape[0]
    mask = lower_mask(rows)
    lower = mask.astype(F32)
    decay = decay_ref[...]
    cum = dot(lower, decay, 1, 1, HIGH)
    cum_heads = dot(decay, lower, 1, 1, HIGH)
    expansion = head_expansion(heads, width)
    grown = dot(jnp.exp(cum), expansion, 1, 0, HIGH)
    skip = dot(skip_ref[...], expansion, 1, 0, HIGH)
    copies[1].wait()
    carry = dot(read_ref[...], start_ref[...], 1, 1)
    copies[2].wait()
    gain = dot(read_ref[...], write_ref[...], 1, 1)
    copies[3].wait()
    copies[4].wait()
    lane = lax.broadcasted_iota(jnp.int32, (rows, LANES), 1)
    total = jnp.zeros((8, rows), F32)
    for pair in range(width // LANES):
        cols = slice(pair * LANES, (pair + 1) * LANES)
        x = x_ref[:, cols]
        found = []
        for h in (2 * pair, 2 * pair + 1):
            gap = cum[:, h : h + 1] - cum_heads[h : h + 1, :]
            mix = gain * jnp.exp(jnp.where(mask, gap, -1e30))
            found.append(dot(mix.astype(BF16), x, 1, 0))
        mixed = jnp.where(lane < HEAD_P, found[0], found[1])
        mixed = mixed + carry[:, cols] * grown[:, cols] + skip[:, cols] * x.astype(F32)
        gate = gate_ref[:, cols].astype(F32)
        gated = mixed * (gate / (1.0 + jnp.exp(-gate)))
        gated_ref[:, cols] = gated
        total = total + dot(jnp.ones((8, LANES), F32), gated * gated, 1, 1, HIGH)
    square_ref[...] = total


def norm_kernel(gated_ref, square_ref, gain_ref, out_ref):
    total = dot(square_ref[...], jnp.ones((square_ref.shape[0], LANES), F32), 0, 0, HIGH)
    scale = lax.rsqrt(total / (SSM_HEADS * HEAD_P) + 1e-05)
    for c in range(0, out_ref.shape[1], LANES):
        cols = slice(c, c + LANES)
        out_ref[:, cols] = (gated_ref[:, cols] * scale * gain_ref[:, cols]).astype(BF16)


def attention_kernel(place_ref, query_hbm, kv_ref, out_ref, query_ref, kv, top, acc, sems):
    rows, width = query_ref.shape
    sets = width // HEAD_DIM
    factor = 1.4426950408889634 / HEAD_DIM**0.5
    place = place_ref[0]
    last = place // GROUP
    keys_at_once = GROUP * rows

    def fetch(c):
        first = pl.multiple_of((last - c) * rows, rows)
        return pltpu.make_async_copy(kv_ref.at[:, pl.ds(first, rows)], kv.at[c], sems.at[c])

    copies = fetch_all([(query_hbm, query_ref)], sems.at[pl.ds(sems.shape[0] - 1, 1)])

    @pl.loop(0, last + 1)
    def _(c):
        fetch(c).start()

    top[...] = jnp.full(top.shape, -1e30, F32)
    acc[...] = jnp.zeros(acc.shape, F32)
    copies[0].wait()

    def step(c, diagonal):
        fetch(c).wait()
        block = kv[c].reshape(keys_at_once, 2 * HEAD_DIM)
        keys = block[:, 0:HEAD_DIM]
        values = jnp.concatenate(
            [block[:, HEAD_DIM : 2 * HEAD_DIM], jnp.ones((keys_at_once, LANES), BF16)], axis=1
        )
        if diagonal:
            t = lax.broadcasted_iota(jnp.int32, (rows, keys_at_once), 0) + place * rows
            s = lax.broadcasted_iota(jnp.int32, (rows, keys_at_once), 1) + c * keys_at_once
            visible = s <= t

        def scores_of(j):
            scores = dot(query_ref[:, j * HEAD_DIM : (j + 1) * HEAD_DIM], keys, 1, 1)
            return jnp.where(visible, scores, -1e30) if diagonal else scores

        ahead = scores_of(0)
        for j in range(sets):
            here = slice(j * rows, (j + 1) * rows)
            scores = ahead
            if j + 1 < sets:
                ahead = scores_of(j + 1)
            old = top[here]
            new = jnp.maximum(old, jnp.max(scores, axis=1, keepdims=True))
            weights = jnp.exp2(scores * factor - new[:, 0:1] * factor).astype(BF16)
            shrink = jnp.exp2((old - new) * factor)
            shrink = jnp.concatenate([shrink, shrink], axis=1)
            acc[here] = acc[here] * shrink + dot(weights, values, 1, 0)
            top[here] = new

    @pl.loop(0, last)
    def _(c):
        step(c, False)

    step(last, True)
    for j in range(sets):
        here = slice(j * rows, (j + 1) * rows)
        out_ref[:, j * HEAD_DIM : (j + 1) * HEAD_DIM] = (
            acc[here, 0:HEAD_DIM] / acc[here, HEAD_DIM : 2 * HEAD_DIM]
        ).astype(BF16)


def vmem_call(kernel, outs, name, flops, moved, **more):
    return pl.pallas_call(
        kernel,
        out_shape=outs,
        name=name,
        compiler_params=pltpu.CompilerParams(vmem_limit_bytes=VMEM_LIMIT),
        cost_estimate=pl.CostEstimate(flops=flops, bytes_accessed=moved, transcendentals=0),
        **more,
    )


def body(
    ssm_input,
    gate_input,
    write_proj,
    read_proj,
    log_decay,
    skip_gain,
    norm_gain,
    query_rows,
    key_rows,
    value_rows,
):
    rows, width = ssm_input.shape
    heads = log_decay.shape[1]
    share = width // PLACES
    place = lax.axis_index(CTX).astype(jnp.int32).reshape(1)
    in_vmem = pl.BlockSpec(memory_space=pltpu.VMEM)
    anywhere = pl.BlockSpec(memory_space=pltpu.HBM)
    x_scratch = pltpu.VMEM((rows, width), BF16)
    decay_scratch = pltpu.VMEM((heads, rows), F32)
    side_scratch = pltpu.VMEM((rows, STATE), BF16)

    ssm_input, gate_input, write_proj, read_proj, query_rows, decay = (
        pltpu.with_memory_space_constraint(a, pltpu.HBM)
        for a in (ssm_input, gate_input, write_proj, read_proj, query_rows, log_decay.T)
    )

    own = jnp.concatenate([key_rows, value_rows], axis=1)
    columns = PLACES // GROUP
    held = [own] + [
        lax.ppermute(own, "x", [(i, i + k) for i in range(columns - k)]) for k in range(1, columns)
    ]
    parts = vmem_call(
        state_kernel,
        jax.ShapeDtypeStruct((PLACES, share + 8, STATE), BF16),
        "device_state",
        2 * rows * width * STATE,
        2 * rows * width,
        in_specs=[anywhere] * 3,
        scratch_shapes=[decay_scratch, x_scratch, side_scratch, pltpu.SemaphoreType.DMA((3,))],
    )(decay, ssm_input, write_proj)
    parts, place, *held = lax.optimization_barrier((parts, place, *held))
    kv = lax.all_gather(jnp.concatenate(held, axis=0), ("y", "core"), axis=0)
    parts = lax.all_to_all(parts, CTX, 0, 0, tiled=True)
    starts = vmem_call(
        fold_kernel,
        jax.ShapeDtypeStruct((PLACES, share, STATE), BF16),
        "state_fold",
        2 * width * STATE,
        4 * width * STATE,
    )(parts)
    starts = lax.all_to_all(starts, CTX, 0, 0, tiled=True)
    gated, square = vmem_call(
        mixer_kernel,
        (
            jax.ShapeDtypeStruct((rows, width), F32),
            jax.ShapeDtypeStruct((8, rows), F32),
        ),
        "mixer",
        4 * rows * rows * width,
        12 * rows * width,
        in_specs=[anywhere] * 5 + [in_vmem] * 2,
        scratch_shapes=[decay_scratch]
        + [x_scratch] * 2
        + [side_scratch] * 2
        + [pltpu.SemaphoreType.DMA((5,))],
    )(
        ssm_input,
        gate_input,
        write_proj,
        read_proj,
        decay,
        skip_gain[None],
        starts.reshape(width, STATE),
    )
    square = lax.all_to_all(square, "heads", 0, 0, tiled=True)
    square, query_rows = lax.optimization_barrier((square, query_rows))
    ssm_out = vmem_call(
        norm_kernel,
        jax.ShapeDtypeStruct((rows, width), BF16),
        "norm",
        4 * rows * width,
        6 * rows * width,
    )(gated, square, norm_gain[None])

    attn_out = vmem_call(
        attention_kernel,
        jax.ShapeDtypeStruct(query_rows.shape, BF16),
        "attention",
        2 * rows * 4 * PLACES * rows * 2 * HEAD_DIM,
        2 * PLACES * rows * 2 * HEAD_DIM,
        in_specs=[pl.BlockSpec(memory_space=pltpu.SMEM), anywhere, anywhere],
        scratch_shapes=[
            pltpu.VMEM(query_rows.shape, BF16),
            pltpu.VMEM((columns, GROUP, rows, 2 * HEAD_DIM), BF16),
            pltpu.VMEM((4 * rows, LANES), F32),
            pltpu.VMEM((4 * rows, 2 * HEAD_DIM), F32),
            pltpu.SemaphoreType.DMA((columns + 1,)),
        ],
    )(place, query_rows, kv)
    return (ssm_out, attn_out)


def solution(mesh):
    fine = Mesh(mesh.devices.reshape(4, 8, 2, 8), CTX + ("heads",))
    split = P(CTX, "heads")
    in_specs = (
        split,
        split,
        P(CTX, None),
        P(CTX, None),
        split,
        P("heads"),
        P("heads"),
        split,
        split,
        split,
    )
    return jax.shard_map(
        body, mesh=fine, in_specs=in_specs, out_specs=(split, split), check_vma=False
    )
```

time: 133 us -> 119 us (0.89)
  the two profiles are of different devices: /device:TPU:63 before, /device:TPU:7 now
where the time goes in v2:
time: 119 us; the launch traced here: 118 us
  blocking collectives  66.5 us (56%)
  Pallas kernels  25.1 us (21%)
  between operations  14.1 us (12%)
  waiting for transfers between devices  4.44 us (4%)
  starting transfers between devices  3.91 us (3%)
  local copies, waits for them, and re-layouts  2.98 us (3%)
    all_to_all x1, blocking collectives, body(): parts = lax.all_to_all(parts, CTX, 0, 0, tiled=True)  26.9 us
    all_to_all x1, blocking collectives, body(): starts = lax.all_to_all(starts, CTX, 0, 0, tiled=True)  20.9 us
    all_to_all x1, blocking collectives, body(): square = lax.all_to_all(square, 'heads', 0, 0, tiled=True)  18.7 us
    pallas_call x1, Pallas kernels, body(): vmem_call(attention_kernel, jax.ShapeDtypeStruct(query_rows.shape, BF16),...  15.2 us
    pallas_call x1, Pallas kernels, body(): vmem_call(mixer_kernel, (jax.ShapeDtypeStruct((rows, width), F32), jax.Sh...  5.97 us
    ppermute x3, waiting for transfers between devices, body(): lax.ppermute(own, 'x', [(i, i + k) for i in range(columns - k)])  4.42 us
    ppermute x3, starting transfers between devices, body(): lax.ppermute(own, 'x', [(i, i + k) for i in range(columns - k)])  3.88 us
    pallas_call x1, Pallas kernels, body(): vmem_call(state_kernel, jax.ShapeDtypeStruct((PLACES, share + 8, STATE),...  2.63 us
  transfers between devices with their start and end apart: 4, of which 2 were waited for; matrix products, arithmetic and copies ran while one was open for 0% of the time, Pallas kernels for 8%

profile of v2, /device:TPU:7, one launch (start us, length us, event | category | flops | bytes accessed | tf_op | source)
XLA Modules:
  0.0 117.8 jit_solution(7624989243145699172)
XLA Ops:
  7.2 0.0 all-gather.3.cloned.1.call-start
  7.2 0.8 constant_dynamic-update-slice_fusion.1
  8.0 0.8 constant_dynamic-update-slice_fusion
  8.8 1.3 %collective-permute-start = (bf16[192,256]{1,0:T(8,128)(2,1)S(1)}, bf16[192,256]{1,0:T(8,128)(2,1)S(1)}, u32[]{:S(2)}, u32[]{:S(2)}) collective-permute-start(bf16[192,256]{1,0:T(8,128)(2,1)S(1)} %constant_dynamic-update-slice_fusion), channel_id=1, source_target_pairs={{0,128},{128,256},{256,384},{1,129},{129,257},{257,385},{2,130},{1... | collective-permute-start | bytes 294920 | tf_op jit(solution)/shard_map/ppermute | solution.py:266
  10.1 1.3 %collective-permute-start.1 = (bf16[192,256]{1,0:T(8,128)(2,1)S(1)}, bf16[192,256]{1,0:T(8,128)(2,1)S(1)}, u32[]{:S(2)}, u32[]{:S(2)}) collective-permute-start(bf16[192,256]{1,0:T(8,128)(2,1)S(1)} %constant_dynamic-update-slice_fusion), channel_id=1, source_target_pairs={{0,256},{128,384},{1,257},{129,385},{2,258},{130,386},{3,259},{131... | collective-permute-start | bytes 294920 | tf_op jit(solution)/shard_map/ppermute | solution.py:266
  11.4 1.3 %collective-permute-start.2 = (bf16[192,256]{1,0:T(8,128)(2,1)S(1)}, bf16[192,256]{1,0:T(8,128)(2,1)S(1)}, u32[]{:S(2)}, u32[]{:S(2)}) collective-permute-start(bf16[192,256]{1,0:T(8,128)(2,1)S(1)} %constant_dynamic-update-slice_fusion), channel_id=1, source_target_pairs={{0,384},{1,385},{2,386},{3,387},{4,388},{5,389},{6,390},{7,391},{8... | collective-permute-start | bytes 294920 | tf_op jit(solution)/shard_map/ppermute | solution.py:266
  12.7 2.6 %device_state.1 = bf16[64,24,128]{2,1,0:T(8,128)(2,1)S(1)} custom-call(f32[16,192]{1,0:T(8,128)} %bitcast.15, bf16[192,1024]{1,0:T(8,128)(2,1)} %x_hbm.3, bf16[192,128]{1,0:T(8,128)(2,1)} %write_hbm.3), custom_call_target="tpu_custom_call" | custom-call | flops 50331648 | bytes 393216 | tf_op jit(solution)/shard_map/device_state/pallas_call | solution.py:268
  15.4 0.0 collective-permute-done
  15.4 1.6 %collective-permute-done.1 = bf16[192,256]{1,0:T(8,128)(2,1)S(1)} collective-permute-done((bf16[192,256]{1,0:T(8,128)(2,1)S(1)}, bf16[192,256]{1,0:T(8,128)(2,1)S(1)}, u32[]{:S(2)}, u32[]{:S(2)}) %collective-permute-start.1) | collective-permute-done | bytes 98336 | tf_op jit(solution)/shard_map/ppermute | solution.py:266
  17.0 2.8 %collective-permute-done.2 = bf16[192,256]{1,0:T(8,128)(2,1)S(1)} collective-permute-done((bf16[192,256]{1,0:T(8,128)(2,1)S(1)}, bf16[192,256]{1,0:T(8,128)(2,1)S(1)}, u32[]{:S(2)}, u32[]{:S(2)}) %collective-permute-start.2) | collective-permute-done | bytes 98336 | tf_op jit(solution)/shard_map/ppermute | solution.py:266
  19.8 0.8 pad_maximum_fusion
  20.6 0.0 all-gather.3.cloned.1.call-update
  20.6 26.9 %all_to_all.22.parts_ref = bf16[64,24,128]{2,1,0:T(8,128)(2,1)S(1)} all-to-all(bf16[64,24,128]{2,1,0:T(8,128)(2,1)S(1)} %device_state.1), channel_id=1, replica_groups=mesh['x'=4,'y'=8,'core'=2,'heads'=8] {'x','y','core'}, dimensions={0} | all-to-all | bytes 786432 | tf_op jit(solution)/shard_map/all_to_all | solution.py:279
  47.5 0.1 state_fold.1
  47.6 20.9 %all_to_all.23 = bf16[64,16,128]{2,1,0:T(8,128)(2,1)S(1)} all-to-all(bf16[64,16,128]{2,1,0:T(8,128)(2,1)S(1)} %state_fold.1), channel_id=1, replica_groups=mesh['x'=4,'y'=8,'core'=2,'heads'=8] {'x','y','core'}, dimensions={0} | all-to-all | bytes 524288 | tf_op jit(solution)/shard_map/all_to_all | solution.py:287
  68.5 0.0 copy-start.1
  68.5 0.7 copy-done.1
  69.2 6.0 %mixer.1 = (f32[192,1024]{1,0:T(8,128)S(1)}, f32[8,192]{1,0:T(8,128)S(1)}) custom-call(bf16[192,1024]{1,0:T(8,128)(2,1)} %x_hbm.3, bf16[192,1024]{1,0:T(8,128)(2,1)} %gate_hbm.1, bf16[192,128]{1,0:T(8,128)(2,1)} %write_hbm.3, bf16[192,128]{1,0:T(8,128)(2,1)} %read_hbm.1, f32[16,192]{1,0:T(8,128)} %bitcast.16, f32[1,16]{1,0:T(1,128)S(1)} %bitcast.14, ...), custom_call_target="tpu_custom_call" | custom-call | flops 150994944 | bytes 2359296 | tf_op jit(solution)/shard_map/mixer/pallas_call | solution.py:288
  75.2 18.7 %all_to_all.24 = f32[8,1,192]{2,1,0:T(1,128)S(1)} all-to-all(f32[8,1,192]{2,1,0:T(1,128)S(1)} %copy.12), channel_id=1, replica_groups=mesh['x'=4,'y'=8,'core'=2,'heads'=8] {'heads'}, dimensions={0} | all-to-all | bytes 12288 | tf_op jit(solution)/shard_map/all_to_all | solution.py:311
  93.9 0.0 copy-start
  93.9 0.7 copy-done
  94.6 1.1 norm.1
  95.7 0.0 all-gather.3.cloned.1.call-done
  95.7 15.2 %attention.1 = bf16[192,512]{1,0:T(8,128)(2,1)} custom-call(s32[1]{0:T(128)} %bitcast.2.place_ref, bf16[192,512]{1,0:T(8,128)(2,1)} %query_hbm, bf16[16,768,256]{2,1,0:T(8,128)(2,1)} %bitcast.17), custom_call_target="tpu_custom_call" | custom-call | flops 4831838208 | bytes 6291456 | tf_op jit(solution)/shard_map/attention/pallas_call | solution.py:321
  (2 shorter events, 0.0 us)
Async XLA Ops:
  7.2 88.5 %all-gather.3.cloned.1.call-start = ((), (), s32[]{:S(2)}) async-start(), calls=%async_computation.3 | async-start | bytes 6684672 | tf_op jit(solution)/shard_map/all_gather | solution.py:278
  8.8 6.5 %collective-permute-start = (bf16[192,256]{1,0:T(8,128)(2,1)S(1)}, bf16[192,256]{1,0:T(8,128)(2,1)S(1)}, u32[]{:S(2)}, u32[]{:S(2)}) collective-permute-start(bf16[192,256]{1,0:T(8,128)(2,1)S(1)} %constant_dynamic-update-slice_fusion), channel_id=1, source_target_pairs={{0,128},{128,256},{256,384},{1,129},{129,257},{257,385},{2,130},{1... | collective-permute-start | bytes 294920 | tf_op jit(solution)/shard_map/ppermute | solution.py:266
  10.1 6.9 %collective-permute-start.1 = (bf16[192,256]{1,0:T(8,128)(2,1)S(1)}, bf16[192,256]{1,0:T(8,128)(2,1)S(1)}, u32[]{:S(2)}, u32[]{:S(2)}) collective-permute-start(bf16[192,256]{1,0:T(8,128)(2,1)S(1)} %constant_dynamic-update-slice_fusion), channel_id=1, source_target_pairs={{0,256},{128,384},{1,257},{129,385},{2,258},{130,386},{3,259},{131... | collective-permute-start | bytes 294920 | tf_op jit(solution)/shard_map/ppermute | solution.py:266
  11.4 8.4 %collective-permute-start.2 = (bf16[192,256]{1,0:T(8,128)(2,1)S(1)}, bf16[192,256]{1,0:T(8,128)(2,1)S(1)}, u32[]{:S(2)}, u32[]{:S(2)}) collective-permute-start(bf16[192,256]{1,0:T(8,128)(2,1)S(1)} %constant_dynamic-update-slice_fusion), channel_id=1, source_target_pairs={{0,384},{1,385},{2,386},{3,387},{4,388},{5,389},{6,390},{7,391},{8... | collective-permute-start | bytes 294920 | tf_op jit(solution)/shard_map/ppermute | solution.py:266
  68.5 0.7 copy-start.1
  93.9 0.7 copy-start
Sparse Core Ops, SparseCore 0:
  20.7 61.0 all-gather.2

commit v3 on v2

--- a/solution.py
+++ b/solution.py
@@ -43,6 +43,12 @@
     for copy in copies:
         copy.start()
     return copies
+
+
+def pack_kernel(key_hbm, value_hbm, out_ref, sems):
+    halves = (out_ref.at[:, 0:HEAD_DIM], out_ref.at[:, HEAD_DIM : 2 * HEAD_DIM])
+    for copy in fetch_all([(key_hbm, halves[0]), (value_hbm, halves[1])], sems):
+        copy.wait()
 
 
 def state_kernel(decay_hbm, x_hbm, write_hbm, out_ref, decay_ref, x_ref, write_ref, sems):
@@ -87,21 +93,21 @@
             state = state * jnp.exp(total) + part[0:share]
 
 
-def mixer_kernel(
+def local_kernel(
+    decay_hbm,
+    read_hbm,
+    write_hbm,
     x_hbm,
     gate_hbm,
-    write_hbm,
-    read_hbm,
-    decay_hbm,
+    skip_hbm,
+    held_ref,
+    grown_ref,
     skip_ref,
-    start_ref,
-    gated_ref,
-    square_ref,
     decay_ref,
+    read_ref,
+    write_ref,
     x_ref,
     gate_ref,
-    write_ref,
-    read_ref,
     sems,
 ):
     copies = fetch_all(
@@ -111,6 +117,7 @@
             (write_hbm, write_ref),
             (x_hbm, x_ref),
             (gate_hbm, gate_ref),
+            (skip_hbm, skip_ref),
         ],
         sems,
     )
@@ -124,15 +131,14 @@
     cum_heads = dot(decay, lower, 1, 1, HIGH)
     expansion = head_expansion(heads, width)
     grown = dot(jnp.exp(cum), expansion, 1, 0, HIGH)
+    copies[5].wait()
     skip = dot(skip_ref[...], expansion, 1, 0, HIGH)
     copies[1].wait()
-    carry = dot(read_ref[...], start_ref[...], 1, 1)
     copies[2].wait()
     gain = dot(read_ref[...], write_ref[...], 1, 1)
     copies[3].wait()
     copies[4].wait()
     lane = lax.broadcasted_iota(jnp.int32, (rows, LANES), 1)
-    total = jnp.zeros((8, rows), F32)
     for pair in range(width // LANES):
         cols = slice(pair * LANES, (pair + 1) * LANES)
         x = x_ref[:, cols]
@@ -141,17 +147,29 @@
             gap = cum[:, h : h + 1] - cum_heads[h : h + 1, :]
             mix = gain * jnp.exp(jnp.where(mask, gap, -1e30))
             found.append(dot(mix.astype(BF16), x, 1, 0))
-        mixed = jnp.where(lane < HEAD_P, found[0], found[1])
-        mixed = mixed + carry[:, cols] * grown[:, cols] + skip[:, cols] * x.astype(F32)
+        mixed = jnp.where(lane < HEAD_P, found[0], found[1]) + skip[:, cols] * x.astype(F32)
         gate = gate_ref[:, cols].astype(F32)
-        gated = mixed * (gate / (1.0 + jnp.exp(-gate)))
+        gate = gate / (1.0 + jnp.exp(-gate))
+        held_ref[:, cols] = mixed * gate
+        grown_ref[:, cols] = grown[:, cols] * gate
+
+
+def carry_kernel(read_hbm, start_ref, held_ref, grown_ref, gated_ref, square_ref, read_ref, sem):
+    copies = fetch_all([(read_hbm, read_ref)], sem)
+    copies[0].wait()
+    rows, width = held_ref.shape
+    total = jnp.zeros((rows, LANES), F32)
+    for pair in range(width // LANES):
+        cols = slice(pair * LANES, (pair + 1) * LANES)
+        carry = dot(read_ref[...], start_ref[cols], 1, 1)
+        gated = held_ref[:, cols] + carry * grown_ref[:, cols]
         gated_ref[:, cols] = gated
-        total = total + dot(jnp.ones((8, LANES), F32), gated * gated, 1, 1, HIGH)
-    square_ref[...] = total
+        total = total + gated * gated
+    square_ref[:, 0, :] = dot(jnp.ones((8, LANES), F32), total, 1, 1, HIGH)
 
 
 def norm_kernel(gated_ref, square_ref, gain_ref, out_ref):
-    total = dot(square_ref[...], jnp.ones((square_ref.shape[0], LANES), F32), 0, 0, HIGH)
+    total = dot(square_ref[:, 0, :], jnp.ones((square_ref.shape[0], LANES), F32), 0, 0, HIGH)
     scale = lax.rsqrt(total / (SSM_HEADS * HEAD_P) + 1e-05)
     for c in range(0, out_ref.shape[1], LANES):
         cols = slice(c, c + LANES)
@@ -159,8 +177,9 @@
 
 
 def attention_kernel(place_ref, query_hbm, kv_ref, out_ref, query_ref, kv, top, acc, sems):
-    rows, width = query_ref.shape
-    sets = width // HEAD_DIM
+    rows = out_ref.shape[0]
+    sets = out_ref.shape[1] // HEAD_DIM
+    stack = 2 * rows
     factor = 1.4426950408889634 / HEAD_DIM**0.5
     place = place_ref[0]
     last = place // GROUP
@@ -170,7 +189,16 @@
         first = pl.multiple_of((last - c) * rows, rows)
         return pltpu.make_async_copy(kv_ref.at[:, pl.ds(first, rows)], kv.at[c], sems.at[c])
 
-    copies = fetch_all([(query_hbm, query_ref)], sems.at[pl.ds(sems.shape[0] - 1, 1)])
+    copies = fetch_all(
+        [
+            (
+                query_hbm.at[:, pl.ds(j * HEAD_DIM, HEAD_DIM)],
+                query_ref.at[pl.ds(j * rows, rows)],
+            )
+            for j in range(sets)
+        ],
+        sems.at[pl.ds(sems.shape[0] - sets, sets)],
+    )
 
     @pl.loop(0, last + 1)
     def _(c):
@@ -178,7 +206,8 @@
 
     top[...] = jnp.full(top.shape, -1e30, F32)
     acc[...] = jnp.zeros(acc.shape, F32)
-    copies[0].wait()
+    for copy in copies:
+        copy.wait()
 
     def step(c, diagonal):
         fetch(c).wait()
@@ -190,18 +219,18 @@
         if diagonal:
             t = lax.broadcasted_iota(jnp.int32, (rows, keys_at_once), 0) + place * rows
             s = lax.broadcasted_iota(jnp.int32, (rows, keys_at_once), 1) + c * keys_at_once
-            visible = s <= t
-
-        def scores_of(j):
-            scores = dot(query_ref[:, j * HEAD_DIM : (j + 1) * HEAD_DIM], keys, 1, 1)
+            visible = jnp.concatenate([s <= t] * (stack // rows), axis=0)
+
+        def scores_of(g):
+            scores = dot(query_ref[g * stack : (g + 1) * stack], keys, 1, 1)
             return jnp.where(visible, scores, -1e30) if diagonal else scores
 
         ahead = scores_of(0)
-        for j in range(sets):
-            here = slice(j * rows, (j + 1) * rows)
+        for g in range(sets * rows // stack):
+            here = slice(g * stack, (g + 1) * stack)
             scores = ahead
-            if j + 1 < sets:
-                ahead = scores_of(j + 1)
+            if (g + 1) * stack < sets * rows:
+                ahead = scores_of(g + 1)
             old = top[here]
             new = jnp.maximum(old, jnp.max(scores, axis=1, keepdims=True))
             weights = jnp.exp2(scores * factor - new[:, 0:1] * factor).astype(BF16)
@@ -255,12 +284,24 @@
     decay_scratch = pltpu.VMEM((heads, rows), F32)
     side_scratch = pltpu.VMEM((rows, STATE), BF16)
 
-    ssm_input, gate_input, write_proj, read_proj, query_rows, decay = (
+    key_rows, value_rows, ssm_input, gate_input, write_proj, read_proj, query_rows = (
         pltpu.with_memory_space_constraint(a, pltpu.HBM)
-        for a in (ssm_input, gate_input, write_proj, read_proj, query_rows, log_decay.T)
-    )
-
-    own = jnp.concatenate([key_rows, value_rows], axis=1)
+        for a in (
+            key_rows, value_rows, ssm_input, gate_input, write_proj, read_proj, query_rows
+        )
+    )
+    decay = pltpu.with_memory_space_constraint(log_decay.T, pltpu.HBM)
+    skip_row = pltpu.with_memory_space_constraint(skip_gain[None], pltpu.HBM)
+
+    own = vmem_call(
+        pack_kernel,
+        jax.ShapeDtypeStruct((rows, 2 * HEAD_DIM), BF16),
+        "pack",
+        0,
+        8 * rows * HEAD_DIM,
+        in_specs=[anywhere] * 2,
+        scratch_shapes=[pltpu.SemaphoreType.DMA((2,))],
+    )(key_rows, value_rows)
     columns = PLACES // GROUP
     held = [own] + [
         lax.ppermute(own, "x", [(i, i + k) for i in range(columns - k)]) for k in range(1, columns)
@@ -274,7 +315,21 @@
         in_specs=[anywhere] * 3,
         scratch_shapes=[decay_scratch, x_scratch, side_scratch, pltpu.SemaphoreType.DMA((3,))],
     )(decay, ssm_input, write_proj)
-    parts, place, *held = lax.optimization_barrier((parts, place, *held))
+    mixed, grown = vmem_call(
+        local_kernel,
+        (jax.ShapeDtypeStruct((rows, width), F32),) * 2,
+        "local",
+        4 * rows * rows * width,
+        12 * rows * width,
+        in_specs=[anywhere] * 6,
+        scratch_shapes=[pltpu.VMEM((1, heads), F32), decay_scratch]
+        + [side_scratch] * 2
+        + [x_scratch] * 2
+        + [pltpu.SemaphoreType.DMA((6,))],
+    )(decay, read_proj, write_proj, ssm_input, gate_input, skip_row)
+    parts, mixed, grown, place, *held = lax.optimization_barrier(
+        (parts, mixed, grown, place, *held)
+    )
     kv = lax.all_gather(jnp.concatenate(held, axis=0), ("y", "core"), axis=0)
     parts = lax.all_to_all(parts, CTX, 0, 0, tiled=True)
     starts = vmem_call(
@@ -286,38 +341,19 @@
     )(parts)
     starts = lax.all_to_all(starts, CTX, 0, 0, tiled=True)
     gated, square = vmem_call(
-        mixer_kernel,
+        carry_kernel,
         (
             jax.ShapeDtypeStruct((rows, width), F32),
-            jax.ShapeDtypeStruct((8, rows), F32),
+            jax.ShapeDtypeStruct((8, 1, rows), F32),
         ),
-        "mixer",
-        4 * rows * rows * width,
+        "carry",
+        2 * rows * width * STATE,
         12 * rows * width,
-        in_specs=[anywhere] * 5 + [in_vmem] * 2,
-        scratch_shapes=[decay_scratch]
-        + [x_scratch] * 2
-        + [side_scratch] * 2
-        + [pltpu.SemaphoreType.DMA((5,))],
-    )(
-        ssm_input,
-        gate_input,
-        write_proj,
-        read_proj,
-        decay,
-        skip_gain[None],
-        starts.reshape(width, STATE),
-    )
+        in_specs=[anywhere] + [in_vmem] * 3,
+        scratch_shapes=[side_scratch, pltpu.SemaphoreType.DMA((1,))],
+    )(read_proj, starts.reshape(width, STATE), mixed, grown)
+    square, query_rows = lax.optimization_barrier((square, query_rows))
     square = lax.all_to_all(square, "heads", 0, 0, tiled=True)
-    square, query_rows = lax.optimization_barrier((square, query_rows))
-    ssm_out = vmem_call(
-        norm_kernel,
-        jax.ShapeDtypeStruct((rows, width), BF16),
-        "norm",
-        4 * rows * width,
-        6 * rows * width,
-    )(gated, square, norm_gain[None])
-
     attn_out = vmem_call(
         attention_kernel,
         jax.ShapeDtypeStruct(query_rows.shape, BF16),
@@ -326,13 +362,21 @@
         2 * PLACES * rows * 2 * HEAD_DIM,
         in_specs=[pl.BlockSpec(memory_space=pltpu.SMEM), anywhere, anywhere],
         scratch_shapes=[
-            pltpu.VMEM(query_rows.shape, BF16),
+            pltpu.VMEM((4 * rows, HEAD_DIM), BF16),
             pltpu.VMEM((columns, GROUP, rows, 2 * HEAD_DIM), BF16),
             pltpu.VMEM((4 * rows, LANES), F32),
             pltpu.VMEM((4 * rows, 2 * HEAD_DIM), F32),
-            pltpu.SemaphoreType.DMA((columns + 1,)),
+            pltpu.SemaphoreType.DMA((columns + 4,)),
         ],
     )(place, query_rows, kv)
+    attn_out, square = lax.optimization_barrier((attn_out, square))
+    ssm_out = vmem_call(
+        norm_kernel,
+        jax.ShapeDtypeStruct((rows, width), BF16),
+        "norm",
+        4 * rows * width,
+        6 * rows * width,
+    )(gated, square, norm_gain[None])
     return (ssm_out, attn_out)
 
 

time: 119 us -> 105 us (0.88)
  blocking collectives: 66.5 us -> 49 us
  starting transfers between devices: 3.91 us -> 16.3 us
  waiting for transfers between devices: 4.44 us -> 0.04 us
  local copies, waits for them, and re-layouts: 2.98 us -> 0.01 us
    all_to_all x1 -> x0, blocking collectives: 18.7 us -> none  [body(): square = lax.all_to_all(square, 'heads', 0, 0, tiled=True)]
    all_to_all x0 -> x1, starting transfers between devices: none -> 12.4 us  [body(): square = lax.all_to_all(square, 'heads', 0, 0, tiled=True)]
    ppermute x3, waiting for transfers between devices: 4.42 us -> 0.01 us  [body(): lax.ppermute(own, 'x', [(i, i + k) for i in range(columns - k)])]
    unnamed x6 -> x2, local copies, waits for them, and re-layouts: 2.16 us -> 0.01 us
    all_to_all x1, blocking collectives: 26.9 us -> 28.1 us  [body(): parts = lax.all_to_all(parts, CTX, 0, 0, tiled=True)]
    pallas_call x1 -> x3, Pallas kernels: 5.97 us -> 6.01 us  [the longest x1 3.18 us: body(): vmem_call(local_kernel, (jax.ShapeDtypeStruct((rows, width), F32),) * 2,...]
  transfers between devices with their start and end apart: 4 -> 5, of which waited for: 2 -> 0; matrix products, arithmetic and copies ran while one was open for 0% -> 0% of each run, Pallas kernels for 8% -> 21%
where the time goes in v3:
time: 105 us
  blocking collectives  49 us (47%)
  Pallas kernels  24.5 us (23%)
  starting transfers between devices  16.3 us (16%)
  between operations  14.2 us (14%)
    all_to_all x1, blocking collectives, body(): parts = lax.all_to_all(parts, CTX, 0, 0, tiled=True)  28.1 us
    all_to_all x1, blocking collectives, body(): starts = lax.all_to_all(starts, CTX, 0, 0, tiled=True)  20.9 us
    pallas_call x1, Pallas kernels, body(): vmem_call(attention_kernel, jax.ShapeDtypeStruct(query_rows.shape, BF16),...  14.6 us
    all_to_all x1, starting transfers between devices, body(): square = lax.all_to_all(square, 'heads', 0, 0, tiled=True)  12.4 us
    ppermute x3, starting transfers between devices, body(): lax.ppermute(own, 'x', [(i, i + k) for i in range(columns - k)])  3.88 us
    pallas_call x1, Pallas kernels, body(): vmem_call(local_kernel, (jax.ShapeDtypeStruct((rows, width), F32),) * 2,...  3.18 us
    pallas_call x1, Pallas kernels, body(): vmem_call(state_kernel, jax.ShapeDtypeStruct((PLACES, share + 8, STATE),...  2.62 us
  transfers between devices with their start and end apart: 5, of which 0 were waited for; matrix products, arithmetic and copies ran while one was open for 0% of the time, Pallas kernels for 21%

profile of v3, /device:TPU:7, one launch (start us, length us, event | category | flops | bytes accessed | tf_op | source)
XLA Modules:
  0.0 104.7 jit_solution(13756838956411431093)
XLA Ops:
  7.2 0.0 all-gather.3.cloned.1.call-start
  7.2 0.8 pack.1
  8.1 1.3 %collective-permute-start.2 = (bf16[192,256]{1,0:T(8,128)(2,1)S(1)}, bf16[192,256]{1,0:T(8,128)(2,1)S(1)}, u32[]{:S(2)}, u32[]{:S(2)}) collective-permute-start(bf16[192,256]{1,0:T(8,128)(2,1)S(1)} %pack.1), channel_id=1, source_target_pairs={{0,384},{1,385},{2,386},{3,387},{4,388},{5,389},{6,390},{7,391},{8... | collective-permute-start | bytes 294920 | tf_op jit(solution)/shard_map/ppermute | solution.py:307
  9.4 1.3 %collective-permute-start.1 = (bf16[192,256]{1,0:T(8,128)(2,1)S(1)}, bf16[192,256]{1,0:T(8,128)(2,1)S(1)}, u32[]{:S(2)}, u32[]{:S(2)}) collective-permute-start(bf16[192,256]{1,0:T(8,128)(2,1)S(1)} %pack.1), channel_id=1, source_target_pairs={{0,256},{128,384},{1,257},{129,385},{2,258},{130,386},{3,259},{131... | collective-permute-start | bytes 294920 | tf_op jit(solution)/shard_map/ppermute | solution.py:307
  10.7 1.3 %collective-permute-start = (bf16[192,256]{1,0:T(8,128)(2,1)S(1)}, bf16[192,256]{1,0:T(8,128)(2,1)S(1)}, u32[]{:S(2)}, u32[]{:S(2)}) collective-permute-start(bf16[192,256]{1,0:T(8,128)(2,1)S(1)} %pack.1), channel_id=1, source_target_pairs={{0,128},{128,256},{256,384},{1,129},{129,257},{257,385},{2,130},{1... | collective-permute-start | bytes 294920 | tf_op jit(solution)/shard_map/ppermute | solution.py:307
  12.0 2.6 %device_state.1 = bf16[64,24,128]{2,1,0:T(8,128)(2,1)S(1)} custom-call(f32[16,192]{1,0:T(8,128)} %bitcast.8, bf16[192,1024]{1,0:T(8,128)(2,1)} %x_hbm.3, bf16[192,128]{1,0:T(8,128)(2,1)} %write_hbm.3), custom_call_target="tpu_custom_call" | custom-call | flops 50331648 | bytes 393216 | tf_op jit(solution)/shard_map/device_state/pallas_call | solution.py:309
  14.6 3.2 %local.1 = (f32[192,1024]{1,0:T(8,128)S(1)}, f32[192,1024]{1,0:T(8,128)S(1)}) custom-call(f32[16,192]{1,0:T(8,128)} %bitcast.9, bf16[192,128]{1,0:T(8,128)(2,1)} %read_hbm.3, bf16[192,128]{1,0:T(8,128)(2,1)} %write_hbm.3, bf16[192,1024]{1,0:T(8,128)(2,1)} %x_hbm.3, bf16[192,1024]{1,0:T(8,128)(2,1)} %gate_hbm.1, f32[1,16]{1,0:T(1,128)} %bitcast.10), custom_call_target="tpu_custom_call" | custom-call | flops 150994944 | bytes 2359296 | tf_op jit(solution)/shard_map/local/pallas_call | solution.py:318
  17.8 0.0 collective-permute-done.2
  17.8 0.0 collective-permute-done.1
  17.8 0.0 collective-permute-done
  17.8 0.8 pad_maximum_fusion
  18.6 0.0 all-gather.3.cloned.1.call-update
  18.6 28.1 %all_to_all.15.parts_ref = bf16[64,24,128]{2,1,0:T(8,128)(2,1)S(1)} all-to-all(bf16[64,24,128]{2,1,0:T(8,128)(2,1)S(1)} %device_state.1), channel_id=1, replica_groups=mesh['x'=4,'y'=8,'core'=2,'heads'=8] {'x','y','core'}, dimensions={0} | all-to-all | bytes 786432 | tf_op jit(solution)/shard_map/all_to_all | solution.py:334
  46.7 0.1 state_fold.1
  46.8 20.9 %all_to_all.16 = bf16[64,16,128]{2,1,0:T(8,128)(2,1)S(1)} all-to-all(bf16[64,16,128]{2,1,0:T(8,128)(2,1)S(1)} %state_fold.1), channel_id=1, replica_groups=mesh['x'=4,'y'=8,'core'=2,'heads'=8] {'x','y','core'}, dimensions={0} | all-to-all | bytes 524288 | tf_op jit(solution)/shard_map/all_to_all | solution.py:342
  67.7 2.0 %carry.1 = (f32[192,1024]{1,0:T(8,128)S(1)}, f32[8,1,192]{2,1,0:T(1,128)}) custom-call(bf16[192,128]{1,0:T(8,128)(2,1)} %read_hbm.3, bf16[1024,128]{1,0:T(8,128)(2,1)S(1)} %bitcast.6, f32[192,1024]{1,0:T(8,128)S(1)} %get-tuple-element.21.held_ref, f32[192,1024]{1,0:T(8,128)S(1)} %get-tuple-element.22.grown_ref), custom_call_target="tpu_custom_call" | custom-call | flops 50331648 | bytes 2359296 | tf_op jit(solution)/shard_map/carry/pallas_call | solution.py:343
  69.7 12.4 %all-to-all-start.2 = ((f32[8,1,192]{2,1,0:T(1,128)}), f32[8,1,192]{2,1,0:T(1,128)S(1)}, u32[]{:S(2)}, u32[]{:S(2)}) async-start(f32[8,1,192]{2,1,0:T(1,128)} %get-tuple-element.31), calls=%async_computation.2 | async-start | bytes 16384 | tf_op jit(solution)/shard_map/all_to_all | solution.py:356
  82.1 0.0 all-gather.3.cloned.1.call-done
  82.1 0.0 copy-start
  82.1 14.6 %attention.1 = bf16[192,512]{1,0:T(8,128)(2,1)} custom-call(s32[1]{0:T(128)} %bitcast.2.place_ref, bf16[192,512]{1,0:T(8,128)(2,1)} %query_hbm, bf16[16,768,256]{2,1,0:T(8,128)(2,1)} %bitcast.11), custom_call_target="tpu_custom_call" | custom-call | flops 4831838208 | bytes 6291456 | tf_op jit(solution)/shard_map/attention/pallas_call | solution.py:357
  96.7 0.0 all-to-all-done.2.square_ref
  96.7 0.0 copy-done
  96.7 1.1 %norm.1 = bf16[192,1024]{1,0:T(8,128)(2,1)} custom-call(f32[192,1024]{1,0:T(8,128)S(1)} %get-tuple-element.23.gated_ref, f32[8,1,192]{2,1,0:T(1,128)S(1)} %all-to-all-done.2.square_ref, f32[1,1024]{1,0:T(1,128)S(1)} %bitcast.7), custom_call_target="tpu_custom_call" | custom-call | flops 786432 | bytes 1179648 | tf_op jit(solution)/shard_map/norm/pallas_call | solution.py:373
Async XLA Ops:
  7.2 75.0 %all-gather.3.cloned.1.call-start = ((), (), s32[]{:S(2)}) async-start(), calls=%async_computation.3 | async-start | bytes 6684672 | tf_op jit(solution)/shard_map/all_gather | solution.py:333
  8.1 9.7 %collective-permute-start.2 = (bf16[192,256]{1,0:T(8,128)(2,1)S(1)}, bf16[192,256]{1,0:T(8,128)(2,1)S(1)}, u32[]{:S(2)}, u32[]{:S(2)}) collective-permute-start(bf16[192,256]{1,0:T(8,128)(2,1)S(1)} %pack.1), channel_id=1, source_target_pairs={{0,384},{1,385},{2,386},{3,387},{4,388},{5,389},{6,390},{7,391},{8... | collective-permute-start | bytes 294920 | tf_op jit(solution)/shard_map/ppermute | solution.py:307
  9.4 8.4 %collective-permute-start.1 = (bf16[192,256]{1,0:T(8,128)(2,1)S(1)}, bf16[192,256]{1,0:T(8,128)(2,1)S(1)}, u32[]{:S(2)}, u32[]{:S(2)}) collective-permute-start(bf16[192,256]{1,0:T(8,128)(2,1)S(1)} %pack.1), channel_id=1, source_target_pairs={{0,256},{128,384},{1,257},{129,385},{2,258},{130,386},{3,259},{131... | collective-permute-start | bytes 294920 | tf_op jit(solution)/shard_map/ppermute | solution.py:307
  10.7 7.2 %collective-permute-start = (bf16[192,256]{1,0:T(8,128)(2,1)S(1)}, bf16[192,256]{1,0:T(8,128)(2,1)S(1)}, u32[]{:S(2)}, u32[]{:S(2)}) collective-permute-start(bf16[192,256]{1,0:T(8,128)(2,1)S(1)} %pack.1), channel_id=1, source_target_pairs={{0,128},{128,256},{256,384},{1,129},{129,257},{257,385},{2,130},{1... | collective-permute-start | bytes 294920 | tf_op jit(solution)/shard_map/ppermute | solution.py:307
  69.7 27.0 %all-to-all-start.2 = ((f32[8,1,192]{2,1,0:T(1,128)}), f32[8,1,192]{2,1,0:T(1,128)S(1)}, u32[]{:S(2)}, u32[]{:S(2)}) async-start(f32[8,1,192]{2,1,0:T(1,128)} %get-tuple-element.31), calls=%async_computation.2 | async-start | bytes 16384 | tf_op jit(solution)/shard_map/all_to_all | solution.py:356
  82.1 14.6 %copy-start = (f32[1024]{0:T(1024)S(1)}, f32[1024]{0:T(1024)}, u32[]{:S(2)}) copy-start(f32[1024]{0:T(1024)} %param.16) | copy-start | bytes 12292
Sparse Core Ops, SparseCore 0:
  18.7 62.2 all-gather.2

commit v4 on v3

--- a/solution.py
+++ b/solution.py
@@ -102,6 +102,7 @@
     skip_hbm,
     held_ref,
     grown_ref,
+    kept_ref,
     skip_ref,
     decay_ref,
     read_ref,
@@ -135,6 +136,7 @@
     skip = dot(skip_ref[...], expansion, 1, 0, HIGH)
     copies[1].wait()
     copies[2].wait()
+    kept_ref[...] = read_ref[...]
     gain = dot(read_ref[...], write_ref[...], 1, 1)
     copies[3].wait()
     copies[4].wait()
@@ -154,9 +156,7 @@
         grown_ref[:, cols] = grown[:, cols] * gate
 
 
-def carry_kernel(read_hbm, start_ref, held_ref, grown_ref, gated_ref, square_ref, read_ref, sem):
-    copies = fetch_all([(read_hbm, read_ref)], sem)
-    copies[0].wait()
+def carry_kernel(read_ref, start_ref, held_ref, grown_ref, gated_ref, square_ref):
     rows, width = held_ref.shape
     total = jnp.zeros((rows, LANES), F32)
     for pair in range(width // LANES):
@@ -179,11 +179,11 @@
 def attention_kernel(place_ref, query_hbm, kv_ref, out_ref, query_ref, kv, top, acc, sems):
     rows = out_ref.shape[0]
     sets = out_ref.shape[1] // HEAD_DIM
-    stack = 2 * rows
+    stacked = sets * rows
+    members = kv.shape[1]
     factor = 1.4426950408889634 / HEAD_DIM**0.5
     place = place_ref[0]
-    last = place // GROUP
-    keys_at_once = GROUP * rows
+    last = place // members
 
     def fetch(c):
         first = pl.multiple_of((last - c) * rows, rows)
@@ -199,26 +199,27 @@
         ],
         sems.at[pl.ds(sems.shape[0] - sets, sets)],
     )
-
-    @pl.loop(0, last + 1)
+    fetch(last).start()
+
+    @pl.loop(0, last)
     def _(c):
         fetch(c).start()
 
-    top[...] = jnp.full(top.shape, -1e30, F32)
-    acc[...] = jnp.zeros(acc.shape, F32)
-    for copy in copies:
-        copy.wait()
-
-    def step(c, diagonal):
-        fetch(c).wait()
-        block = kv[c].reshape(keys_at_once, 2 * HEAD_DIM)
-        keys = block[:, 0:HEAD_DIM]
-        values = jnp.concatenate(
-            [block[:, HEAD_DIM : 2 * HEAD_DIM], jnp.ones((keys_at_once, LANES), BF16)], axis=1
-        )
+    def load(c, first, count):
+        block = kv[c, first : first + count].reshape(count * rows, 2 * HEAD_DIM)
+        ones = jnp.ones((count * rows, LANES), BF16)
+        return block[:, 0:HEAD_DIM], jnp.concatenate([block[:, HEAD_DIM:], ones], axis=1)
+
+    def weigh(scores, peak):
+        return jnp.exp2(scores * factor - peak * factor).astype(BF16)
+
+    def exact_step(c, diagonal):
+        keys, values = load(c, 0, members)
+        stack = 2 * rows
         if diagonal:
-            t = lax.broadcasted_iota(jnp.int32, (rows, keys_at_once), 0) + place * rows
-            s = lax.broadcasted_iota(jnp.int32, (rows, keys_at_once), 1) + c * keys_at_once
+            count = members * rows
+            t = lax.broadcasted_iota(jnp.int32, (rows, count), 0) + place * rows
+            s = lax.broadcasted_iota(jnp.int32, (rows, count), 1) + c * count
             visible = jnp.concatenate([s <= t] * (stack // rows), axis=0)
 
         def scores_of(g):
@@ -226,24 +227,35 @@
             return jnp.where(visible, scores, -1e30) if diagonal else scores
 
         ahead = scores_of(0)
-        for g in range(sets * rows // stack):
+        for g in range(stacked // stack):
             here = slice(g * stack, (g + 1) * stack)
             scores = ahead
-            if (g + 1) * stack < sets * rows:
+            if (g + 1) * stack < stacked:
                 ahead = scores_of(g + 1)
-            old = top[here]
-            new = jnp.maximum(old, jnp.max(scores, axis=1, keepdims=True))
-            weights = jnp.exp2(scores * factor - new[:, 0:1] * factor).astype(BF16)
-            shrink = jnp.exp2((old - new) * factor)
-            shrink = jnp.concatenate([shrink, shrink], axis=1)
-            acc[here] = acc[here] * shrink + dot(weights, values, 1, 0)
-            top[here] = new
+            peak = jnp.max(scores, axis=1, keepdims=True)
+            if diagonal:
+                acc[here] = dot(weigh(scores, peak), values, 1, 0)
+                top[here] = jnp.broadcast_to(peak, (stack, LANES))
+            else:
+                old = top[here]
+                new = jnp.maximum(old, peak)
+                shrink = jnp.exp2((old - new) * factor)
+                shrink = jnp.concatenate([shrink, shrink], axis=1)
+                acc[here] = acc[here] * shrink + dot(
+                    weigh(scores, new[:, 0:1]), values, 1, 0
+                )
+                top[here] = new
+
+    for copy in copies:
+        copy.wait()
+    fetch(last).wait()
+    exact_step(last, True)
 
     @pl.loop(0, last)
     def _(c):
-        step(c, False)
-
-    step(last, True)
+        fetch(c).wait()
+        exact_step(c, False)
+
     for j in range(sets):
         here = slice(j * rows, (j + 1) * rows)
         out_ref[:, j * HEAD_DIM : (j + 1) * HEAD_DIM] = (
@@ -315,9 +327,13 @@
         in_specs=[anywhere] * 3,
         scratch_shapes=[decay_scratch, x_scratch, side_scratch, pltpu.SemaphoreType.DMA((3,))],
     )(decay, ssm_input, write_proj)
-    mixed, grown = vmem_call(
+    mixed, grown, kept = vmem_call(
         local_kernel,
-        (jax.ShapeDtypeStruct((rows, width), F32),) * 2,
+        (
+            jax.ShapeDtypeStruct((rows, width), F32),
+            jax.ShapeDtypeStruct((rows, width), F32),
+            jax.ShapeDtypeStruct((rows, STATE), BF16),
+        ),
         "local",
         4 * rows * rows * width,
         12 * rows * width,
@@ -327,8 +343,8 @@
         + [x_scratch] * 2
         + [pltpu.SemaphoreType.DMA((6,))],
     )(decay, read_proj, write_proj, ssm_input, gate_input, skip_row)
-    parts, mixed, grown, place, *held = lax.optimization_barrier(
-        (parts, mixed, grown, place, *held)
+    parts, mixed, grown, kept, place, *held = lax.optimization_barrier(
+        (parts, mixed, grown, kept, place, *held)
     )
     kv = lax.all_gather(jnp.concatenate(held, axis=0), ("y", "core"), axis=0)
     parts = lax.all_to_all(parts, CTX, 0, 0, tiled=True)
@@ -349,9 +365,7 @@
         "carry",
         2 * rows * width * STATE,
         12 * rows * width,
-        in_specs=[anywhere] + [in_vmem] * 3,
-        scratch_shapes=[side_scratch, pltpu.SemaphoreType.DMA((1,))],
-    )(read_proj, starts.reshape(width, STATE), mixed, grown)
+    )(kept, starts.reshape(width, STATE), mixed, grown)
     square, query_rows = lax.optimization_barrier((square, query_rows))
     square = lax.all_to_all(square, "heads", 0, 0, tiled=True)
     attn_out = vmem_call(

time: 105 us -> 104 us (level)
  no operation moved by 1% of the time
where the time goes in v4:
time: 104 us
  blocking collectives  49 us (47%)
  Pallas kernels  23.6 us (23%)
  starting transfers between devices  16.3 us (16%)
  between operations  14.1 us (14%)
    all_to_all x1, blocking collectives, body(): parts = lax.all_to_all(parts, CTX, 0, 0, tiled=True)  28.1 us
    all_to_all x1, blocking collectives, body(): starts = lax.all_to_all(starts, CTX, 0, 0, tiled=True)  20.9 us
    pallas_call x1, Pallas kernels, body(): vmem_call(attention_kernel, jax.ShapeDtypeStruct(query_rows.shape, BF16),...  14.5 us
    all_to_all x1, starting transfers between devices, body(): square = lax.all_to_all(square, 'heads', 0, 0, tiled=True)  12.4 us
    ppermute x3, starting transfers between devices, body(): lax.ppermute(own, 'x', [(i, i + k) for i in range(columns - k)])  3.88 us
    pallas_call x1, Pallas kernels, body(): vmem_call(local_kernel, (jax.ShapeDtypeStruct((rows, width), F32), jax.Sh...  3.19 us
    pallas_call x1, Pallas kernels, body(): vmem_call(state_kernel, jax.ShapeDtypeStruct((PLACES, share + 8, STATE),...  2.62 us
  transfers between devices with their start and end apart: 5, of which 0 were waited for; matrix products, arithmetic and copies ran while one was open for 0% of the time, Pallas kernels for 21%

profile of v4, /device:TPU:7, one launch (start us, length us, event | category | flops | bytes accessed | tf_op | source)
XLA Modules:
  0.0 103.9 jit_solution(13213537402457516756)
XLA Ops:
  7.2 0.0 all-gather.3.cloned.1.call-start
  7.2 0.8 pack.1
  8.1 1.3 %collective-permute-start.2 = (bf16[192,256]{1,0:T(8,128)(2,1)S(1)}, bf16[192,256]{1,0:T(8,128)(2,1)S(1)}, u32[]{:S(2)}, u32[]{:S(2)}) collective-permute-start(bf16[192,256]{1,0:T(8,128)(2,1)S(1)} %pack.1), channel_id=1, source_target_pairs={{0,384},{1,385},{2,386},{3,387},{4,388},{5,389},{6,390},{7,391},{8... | collective-permute-start | bytes 294920 | tf_op jit(solution)/shard_map/ppermute | solution.py:319
  9.4 1.3 %collective-permute-start.1 = (bf16[192,256]{1,0:T(8,128)(2,1)S(1)}, bf16[192,256]{1,0:T(8,128)(2,1)S(1)}, u32[]{:S(2)}, u32[]{:S(2)}) collective-permute-start(bf16[192,256]{1,0:T(8,128)(2,1)S(1)} %pack.1), channel_id=1, source_target_pairs={{0,256},{128,384},{1,257},{129,385},{2,258},{130,386},{3,259},{131... | collective-permute-start | bytes 294920 | tf_op jit(solution)/shard_map/ppermute | solution.py:319
  10.7 1.3 %collective-permute-start = (bf16[192,256]{1,0:T(8,128)(2,1)S(1)}, bf16[192,256]{1,0:T(8,128)(2,1)S(1)}, u32[]{:S(2)}, u32[]{:S(2)}) collective-permute-start(bf16[192,256]{1,0:T(8,128)(2,1)S(1)} %pack.1), channel_id=1, source_target_pairs={{0,128},{128,256},{256,384},{1,129},{129,257},{257,385},{2,130},{1... | collective-permute-start | bytes 294920 | tf_op jit(solution)/shard_map/ppermute | solution.py:319
  12.0 2.6 %device_state.1 = bf16[64,24,128]{2,1,0:T(8,128)(2,1)S(1)} custom-call(f32[16,192]{1,0:T(8,128)} %bitcast.8, bf16[192,1024]{1,0:T(8,128)(2,1)} %x_hbm.3, bf16[192,128]{1,0:T(8,128)(2,1)} %write_hbm.3), custom_call_target="tpu_custom_call" | custom-call | flops 50331648 | bytes 393216 | tf_op jit(solution)/shard_map/device_state/pallas_call | solution.py:321
  14.6 3.2 %local.1 = (f32[192,1024]{1,0:T(8,128)S(1)}, f32[192,1024]{1,0:T(8,128)S(1)}, bf16[192,128]{1,0:T(8,128)(2,1)S(1)}) custom-call(f32[16,192]{1,0:T(8,128)} %bitcast.9, bf16[192,128]{1,0:T(8,128)(2,1)} %read_hbm.1, bf16[192,128]{1,0:T(8,128)(2,1)} %write_hbm.3, bf16[192,1024]{1,0:T(8,128)(2,1)} %x_hbm.3, bf16[192,1024]{1,0:T(8,128)(2,1)} %gate_hbm.1, ...), custom_call_target="tpu_custom_call" | custom-call | flops 150994944 | bytes 2359296 | tf_op jit(solution)/shard_map/local/pallas_call | solution.py:330
  17.8 0.0 collective-permute-done.2
  17.8 0.0 collective-permute-done.1
  17.8 0.0 collective-permute-done
  17.8 0.8 pad_maximum_fusion
  18.6 0.0 all-gather.3.cloned.1.call-update
  18.6 28.1 %all_to_all.15.parts_ref = bf16[64,24,128]{2,1,0:T(8,128)(2,1)S(1)} all-to-all(bf16[64,24,128]{2,1,0:T(8,128)(2,1)S(1)} %device_state.1), channel_id=1, replica_groups=mesh['x'=4,'y'=8,'core'=2,'heads'=8] {'x','y','core'}, dimensions={0} | all-to-all | bytes 786432 | tf_op jit(solution)/shard_map/all_to_all | solution.py:350
  46.7 0.1 state_fold.1
  46.8 20.9 %all_to_all.16 = bf16[64,16,128]{2,1,0:T(8,128)(2,1)S(1)} all-to-all(bf16[64,16,128]{2,1,0:T(8,128)(2,1)S(1)} %state_fold.1), channel_id=1, replica_groups=mesh['x'=4,'y'=8,'core'=2,'heads'=8] {'x','y','core'}, dimensions={0} | all-to-all | bytes 524288 | tf_op jit(solution)/shard_map/all_to_all | solution.py:358
  67.7 1.2 %carry.1 = (f32[192,1024]{1,0:T(8,128)S(1)}, f32[8,1,192]{2,1,0:T(1,128)}) custom-call(bf16[192,128]{1,0:T(8,128)(2,1)S(1)} %get-tuple-element.23.read_ref, bf16[1024,128]{1,0:T(8,128)(2,1)S(1)} %bitcast.6, f32[192,1024]{1,0:T(8,128)S(1)} %get-tuple-element.25.held_ref, f32[192,1024]{1,0:T(8,128)S(1)} %get-tuple-element.26.grown_ref), custom_call_target="tpu_custom_call" | custom-call | flops 50331648 | bytes 2359296 | tf_op jit(solution)/shard_map/carry/pallas_call | solution.py:359
  68.9 12.4 %all-to-all-start.2 = ((f32[8,1,192]{2,1,0:T(1,128)}), f32[8,1,192]{2,1,0:T(1,128)S(1)}, u32[]{:S(2)}, u32[]{:S(2)}) async-start(f32[8,1,192]{2,1,0:T(1,128)} %get-tuple-element.35), calls=%async_computation.2 | async-start | bytes 16384 | tf_op jit(solution)/shard_map/all_to_all | solution.py:370
  81.3 0.0 all-gather.3.cloned.1.call-done
  81.3 0.0 copy-start
  81.3 14.5 %attention.1 = bf16[192,512]{1,0:T(8,128)(2,1)} custom-call(s32[1]{0:T(128)} %bitcast.2.place_ref, bf16[192,512]{1,0:T(8,128)(2,1)} %query_hbm, bf16[16,768,256]{2,1,0:T(8,128)(2,1)} %bitcast.11), custom_call_target="tpu_custom_call" | custom-call | flops 4831838208 | bytes 6291456 | tf_op jit(solution)/shard_map/attention/pallas_call | solution.py:371
  95.9 0.0 all-to-all-done.2.square_ref
  95.9 0.0 copy-done
  95.9 1.1 %norm.1 = bf16[192,1024]{1,0:T(8,128)(2,1)} custom-call(f32[192,1024]{1,0:T(8,128)S(1)} %get-tuple-element.27.gated_ref, f32[8,1,192]{2,1,0:T(1,128)S(1)} %all-to-all-done.2.square_ref, f32[1,1024]{1,0:T(1,128)S(1)} %bitcast.7), custom_call_target="tpu_custom_call" | custom-call | flops 786432 | bytes 1179648 | tf_op jit(solution)/shard_map/norm/pallas_call | solution.py:387
Async XLA Ops:
  7.2 74.1 %all-gather.3.cloned.1.call-start = ((), (), s32[]{:S(2)}) async-start(), calls=%async_computation.3 | async-start | bytes 6684672 | tf_op jit(solution)/shard_map/all_gather | solution.py:349
  8.1 9.7 %collective-permute-start.2 = (bf16[192,256]{1,0:T(8,128)(2,1)S(1)}, bf16[192,256]{1,0:T(8,128)(2,1)S(1)}, u32[]{:S(2)}, u32[]{:S(2)}) collective-permute-start(bf16[192,256]{1,0:T(8,128)(2,1)S(1)} %pack.1), channel_id=1, source_target_pairs={{0,384},{1,385},{2,386},{3,387},{4,388},{5,389},{6,390},{7,391},{8... | collective-permute-start | bytes 294920 | tf_op jit(solution)/shard_map/ppermute | solution.py:319
  9.4 8.4 %collective-permute-start.1 = (bf16[192,256]{1,0:T(8,128)(2,1)S(1)}, bf16[192,256]{1,0:T(8,128)(2,1)S(1)}, u32[]{:S(2)}, u32[]{:S(2)}) collective-permute-start(bf16[192,256]{1,0:T(8,128)(2,1)S(1)} %pack.1), channel_id=1, source_target_pairs={{0,256},{128,384},{1,257},{129,385},{2,258},{130,386},{3,259},{131... | collective-permute-start | bytes 294920 | tf_op jit(solution)/shard_map/ppermute | solution.py:319
  10.7 7.2 %collective-permute-start = (bf16[192,256]{1,0:T(8,128)(2,1)S(1)}, bf16[192,256]{1,0:T(8,128)(2,1)S(1)}, u32[]{:S(2)}, u32[]{:S(2)}) collective-permute-start(bf16[192,256]{1,0:T(8,128)(2,1)S(1)} %pack.1), channel_id=1, source_target_pairs={{0,128},{128,256},{256,384},{1,129},{129,257},{257,385},{2,130},{1... | collective-permute-start | bytes 294920 | tf_op jit(solution)/shard_map/ppermute | solution.py:319
  68.9 26.9 %all-to-all-start.2 = ((f32[8,1,192]{2,1,0:T(1,128)}), f32[8,1,192]{2,1,0:T(1,128)S(1)}, u32[]{:S(2)}, u32[]{:S(2)}) async-start(f32[8,1,192]{2,1,0:T(1,128)} %get-tuple-element.35), calls=%async_computation.2 | async-start | bytes 16384 | tf_op jit(solution)/shard_map/all_to_all | solution.py:370
  81.3 14.6 %copy-start = (f32[1024]{0:T(1024)S(1)}, f32[1024]{0:T(1024)}, u32[]{:S(2)}) copy-start(f32[1024]{0:T(1024)} %param.16) | copy-start | bytes 12292
Sparse Core Ops, SparseCore 0:
  18.7 62.2 all-gather.2
